TPU v7x, 128 devices: a whole 4x4x4 slice. The times are simulated.
128 devices in a mesh: sample: 16 (over y, x), col: 8 (over z, core).
Axes of the slice: x: 4, y: 4, z: 4, core: 2. Of those that a mesh axis runs over, the one named last changes fastest.
Arguments:
- block_inputs: bfloat16 [2048, 17, 17, 768], P(('sample', 'col')), may hold values from 0 to 100, as said below
- first_entry: bfloat16 [1, 1, 768, 384], replicated, may hold values from -0.3125 to 0.3125
- first_wide: bfloat16 [3, 3, 192, 320], replicated, may hold values from -0.21875 to 0.21875
- first_row: bfloat16 [1, 7, 192, 192], replicated, may hold values from -0.25 to 0.25
- first_column: bfloat16 [7, 1, 192, 192], replicated, may hold values from -0.25 to 0.25
- first_reduce: bfloat16 [3, 3, 192, 192], replicated, may hold values from -0.21875 to 0.21875
- second_entry: bfloat16 [1, 1, 1280, 1152], replicated, may hold values from -0.25 to 0.25
- second_row: bfloat16 [1, 3, 384, 384], replicated, may hold values from -0.25 to 0.25
- second_column: bfloat16 [3, 1, 384, 384], replicated, may hold values from -0.25 to 0.25
- second_deep: bfloat16 [3, 3, 448, 384], replicated, may hold values from -0.125 to 0.125
- deep_row: bfloat16 [1, 3, 384, 384], replicated, may hold values from -0.25 to 0.25
- deep_column: bfloat16 [3, 1, 384, 384], replicated, may hold values from -0.25 to 0.25
- pool_project: bfloat16 [1, 1, 1280, 192], replicated, may hold values from -0.25 to 0.25
Outputs:
- feature_mean: float32 [2048], replicated
- covariance: float32 [2048, 2048], P('sample', 'col')
Inputs may be any that keep to these rules, and one draw needn't show every extreme that they name: `block_inputs`: nonnegative activations.
All inputs are finite; a program needn't handle non-finite values.
Results may differ from a plain program's by a relative error of at most 0.0003.
Values sent between devices are 32-bit elements; how exact they have to be, the bound alone decides.
No kernel may reach another device: no remote copies, remote signals or barrier semaphores. Data moves between devices by JAX's collectives and lax.ppermute only.
A program may use at most 128 MiB of HBM per device.

v0:
```python
import jax
import jax.numpy as jnp
from jax import lax
from jax.sharding import PartitionSpec as P


def combined_all(part, axis, combine):
    gathered = jax.tree.map(lambda a: lax.all_gather(a, axis), part)

    def take(source):
        return jax.tree.map(lambda a: lax.dynamic_index_in_dim(a, source, 0, False), gathered)

    return lax.fori_loop(
        1, lax.axis_size(axis), lambda source, state: combine(state, take(source)), take(0)
    )


def rectify(inputs, kernel, stride, padding):
    result = lax.conv_general_dilated(
        inputs,
        kernel,
        (stride, stride),
        padding,
        dimension_numbers=("NHWC", "HWIO", "NHWC"),
        preferred_element_type=jnp.float32,
    )
    return jnp.maximum(result, 0.0).astype(jnp.bfloat16)


def spatial_mean(inputs):
    return jnp.mean(inputs.astype(jnp.float32), axis=(1, 2))


def network(
    block_inputs,
    first_entry,
    first_wide,
    first_row,
    first_column,
    first_reduce,
    second_entry,
    second_row,
    second_column,
    second_deep,
    deep_row,
    deep_column,
    pool_project,
):
    no_margin = ((0, 0), (0, 0))
    entry_out = rectify(block_inputs, first_entry, 1, no_margin)
    half_width = first_wide.shape[2]
    wide_out = rectify(entry_out[..., :half_width], first_wide, 2, no_margin)
    tower_out = rectify(entry_out[..., half_width:], first_row, 1, ((0, 0), (3, 3)))
    tower_out = rectify(tower_out, first_column, 1, ((3, 3), (0, 0)))
    tower_out = rectify(tower_out, first_reduce, 2, no_margin)
    maximum = lax.reduce_window(
        block_inputs,
        jnp.array(-jnp.inf, block_inputs.dtype),
        lax.max,
        (1, 3, 3, 1),
        (1, 2, 2, 1),
        "VALID",
    )
    middle = jnp.concatenate([wide_out, tower_out, maximum], axis=3)
    second = rectify(middle, second_entry, 1, no_margin)
    branch_width = second_row.shape[2]
    deep_width = second_deep.shape[2]
    plain_width = second_entry.shape[3] - branch_width - deep_width
    plain_out = second[..., :plain_width]
    branch_in = second[..., plain_width : plain_width + branch_width]
    deep_in = second[..., plain_width + branch_width :]
    row_a = rectify(branch_in, second_row, 1, ((0, 0), (1, 1)))
    col_a = rectify(branch_in, second_column, 1, ((1, 1), (0, 0)))
    deep_out = rectify(deep_in, second_deep, 1, ((1, 1), (1, 1)))
    row_b = rectify(deep_out, deep_row, 1, ((0, 0), (1, 1)))
    col_b = rectify(deep_out, deep_column, 1, ((1, 1), (0, 0)))
    pool_pad = ((0, 0), (1, 1), (1, 1), (0, 0))
    summed = lax.reduce_window(
        middle.astype(jnp.float32),
        jnp.array(0.0, jnp.float32),
        lax.add,
        (1, 3, 3, 1),
        (1, 1, 1, 1),
        pool_pad,
    )
    ones_map = jnp.ones((1, middle.shape[1], middle.shape[2], 1), jnp.float32)
    cell_count = lax.reduce_window(
        ones_map, jnp.array(0.0, jnp.float32), lax.add, (1, 3, 3, 1), (1, 1, 1, 1), pool_pad
    )
    averaged = (summed / cell_count).astype(jnp.bfloat16)
    pooled = rectify(averaged, pool_project, 1, no_margin)
    return jnp.concatenate(
        [
            spatial_mean(plain_out),
            spatial_mean(row_a),
            spatial_mean(col_a),
            spatial_mean(row_b),
            spatial_mean(col_b),
            spatial_mean(pooled),
        ],
        axis=1,
    )


def local(
    block_inputs,
    first_entry,
    first_wide,
    first_row,
    first_column,
    first_reduce,
    second_entry,
    second_row,
    second_column,
    second_deep,
    deep_row,
    deep_column,
    pool_project,
):
    features = network(
        block_inputs,
        first_entry,
        first_wide,
        first_row,
        first_column,
        first_reduce,
        second_entry,
        second_row,
        second_column,
        second_deep,
        deep_row,
        deep_column,
        pool_project,
    )
    gathered = lax.all_gather(features, "col", axis=0, tiled=True)
    width = gathered.shape[1]
    col_width = width // lax.axis_size("col")
    col_start = lax.axis_index("col") * col_width
    row_width = width // lax.axis_size("sample")
    row_start = lax.axis_index("sample") * row_width
    group_images = gathered.shape[0]
    total_images = group_images * lax.axis_size("sample")
    highest = lax.Precision.HIGHEST
    group_mean = jnp.sum(gathered, axis=0) / group_images
    centered = gathered - group_mean
    columns = lax.dynamic_slice_in_dim(centered, col_start, col_width, 1)
    moments = jnp.einsum(
        "nf,nc->fc", centered, columns, precision=highest, preferred_element_type=jnp.float32
    )
    members = jnp.array(group_images, jnp.float32)

    def combine(earlier, latter):
        count_a, mean_a, moment_a = earlier
        count_b, mean_b, moment_b = latter
        count_all = count_a + count_b
        mean_gap = mean_b - mean_a
        gap_columns = lax.dynamic_slice_in_dim(mean_gap, col_start, col_width, 0)
        mean_all = mean_a + mean_gap * (count_b / count_all)
        moment_all = (
            moment_a + moment_b + jnp.outer(mean_gap, gap_columns) * (count_a * count_b / count_all)
        )
        return (count_all, mean_all, moment_all)

    merged_count, feature_mean, merged_moments = combined_all(
        (members, group_mean, moments), "sample", combine
    )
    covariance = lax.dynamic_slice_in_dim(merged_moments, row_start, row_width, 0) / (
        total_images - 1
    )
    return (feature_mean, covariance)


def solution(mesh):
    placed = (
        P(("sample", "col"), None, None, None),
        P(),
        P(),
        P(),
        P(),
        P(),
        P(),
        P(),
        P(),
        P(),
        P(),
        P(),
        P(),
    )
    return jax.shard_map(
        local, mesh=mesh, in_specs=placed, out_specs=(P(), P("sample", "col")), check_vma=False
    )
```

profile of v0, /device:TPU:1, one launch (start us, length us, event | category | flops | bytes accessed | tf_op | source)
XLA Modules:
  0.0 411.1 jit_solution(14171061432312267951)
XLA Ops:
  7.2 5.7 %fusion.26 = bf16[16,8,8,768]{3,0,2,1:T(8,128)(2,1)} fusion(bf16[16,17,17,768]{3,0,2,1:T(8,128)(2,1)} %param.15), kind=kOutput, calls=%fused_computation.51 | output fusion | flops 6291456 | bytes 8675328 | tf_op jit(solution)/shard_map/reduce_window | solution.py:56
  12.9 4.1 maximum_convert_fusion
  17.1 3.0 maximum_convert_fusion.11
  20.1 11.7 %fusion.7 = bf16[16,17,17,192]{3,0,2,1:T(8,128)(2,1)} fusion(bf16[1,7,192,192]{3,2,1,0:T(8,128)(2,1)S(1)} %copy-done.10, bf16[16,17,17,384]{3,0,2,1:T(8,128)(2,1)S(1)} %maximum_convert_fusion), kind=kOutput, calls=%fused_computation.13 | convolution fusion | flops 2145779712 | bytes 4831232 | tf_op jit(solution)/shard_map/conv_general_dilated | solution.py:19
  31.7 9.4 %fusion.14 = bf16[16,8,8,192]{3,0,2,1:T(8,128)(2,1)} fusion(bf16[3,3,192,192]{3,2,1,0:T(8,128)(2,1)} %param.20, bf16[7,1,192,192]{3,2,1,0:T(8,128)(2,1)} %param.19, bf16[16,17,17,192]{3,0,2,1:T(8,128)(2,1)} %fusion.7), kind=kOutput, calls=%fused_computation.31 | convolution fusion | flops 2830089216 | bytes 3348480 | tf_op jit(solution)/shard_map/conv_general_dilated | solution.py:19
  41.1 5.4 %concatenate.6 = bf16[16,8,8,1280]{3,0,2,1:T(8,128)(2,1)} concatenate(bf16[16,8,8,320]{3,0,2,1:T(8,128)(2,1)} %maximum_convert_fusion.11, bf16[16,8,8,192]{3,0,2,1:T(8,128)(2,1)} %fusion.14, bf16[16,8,8,768]{3,0,2,1:T(8,128)(2,1)} %fusion.26), dimensions={3} | concatenate | bytes 5242880 | tf_op jit(solution)/shard_map/concatenate | solution.py:64
  46.5 6.3 %fusion.5 = bf16[16,8,8,1152]{3,0,2,1:T(8,128)(2,1)S(1)} fusion(bf16[16,8,8,1280]{3,0,2,1:T(8,128)(2,1)} %concatenate.6, bf16[1,1,1280,1152]{3,2,1,0:T(8,128)(2,1)} %param.21), kind=kOutput, calls=%fused_computation.11 | convolution fusion | flops 3022258176 | bytes 7929856 | tf_op jit(solution)/shard_map/conv_general_dilated | solution.py:19
  52.9 1.6 multiply_convert_fusion
  54.5 0.9 fusion.17
  55.6 1.5 convert_reduce_fusion.2
  57.1 1.5 convert_reduce_fusion.3
  58.7 4.6 %maximum_convert_fusion.8 = bf16[16,8,8,384]{3,0,2,1:T(8,128)(2,1)S(1)} fusion(bf16[3,3,448,384]{3,2,1,0:T(8,128)(2,1)S(1)} %copy-done, bf16[16,8,8,1152]{3,0,2,1:T(8,128)(2,1)S(1)} %fusion.5), kind=kOutput, calls=%fused_computation.22 | convolution fusion | flops 2665218048 | bytes 4931584 | tf_op jit(solution)/shard_map/conv_general_dilated | solution.py:19
  63.3 1.5 convert_reduce_fusion
  64.8 1.7 convert_reduce_fusion.1
  66.6 0.8 concatenate.7
  67.4 27.1 %all-gather.5.cloned.1.call-done = f32[128,2048]{1,0:T(8,128)} async-done(((f32[16,2048]{1,0:T(8,128)}), f32[128,2048]{1,0:T(8,128)}) %all-gather.5.cloned.1.call-update) | async-done | bytes 1048592 | tf_op jit(solution)/shard_map/all_gather | solution.py:135
  94.5 1.3 reduce_sum.69
  95.8 1.3 broadcast_subtract_fusion
  97.2 3.2 fusion.21
  101.0 0.8 dynamic-update-slice
  101.7 34.3 %all-reduce = f32[16]{0:T(128)S(1)} all-reduce(f32[16]{0:T(128)S(1)} %dynamic-update-slice), channel_id=1, replica_groups=mesh['sample'=16,'col'=8] {'sample'}, use_global_device_ids=true, to_apply=%add | all-reduce | flops 16 | bytes 128
  136.1 17.7 %all-gather = f32[32768]{0:T(1024)S(1)} all-gather(f32[2048]{0:T(1024)S(1)} %broadcast_multiply_fusion.6), channel_id=2, replica_groups=mesh['sample'=16,'col'=8] {'sample'}, dimensions={0}, use_global_device_ids=true | all-gather | bytes 139264 | tf_op jit(solution)/shard_map/all_gather | solution.py:8
  153.9 143.4 %all-gather.7.cloned.1.call-done = f32[32768,256]{1,0:T(8,128)} async-done(((f32[2048,256]{1,0:T(8,128)}), f32[32768,256]{1,0:T(8,128)}) %all-gather.7.cloned.1.call-update) | async-done | bytes 33554448 | tf_op jit(solution)/shard_map/all_gather | solution.py:8
  297.3 3.0 slice.31
  300.3 102.3 %while.21 = (s32[]{:T(128)}, f32[]{:T(128)}, f32[2048]{0:T(1024)S(1)}, f32[2048,256]{1,0:T(8,128)}, f32[16]{0:T(128)S(1)}, /*index=5*/f32[16,2048]{1,0:T(8,128)S...) while((s32[]{:T(128)}, f32[]{:T(128)}, f32[2048]{0:T(1024)S(1)}, ...), condition=%wide.region_10.11_spmd, body=%wide.region_9.0_spmd.sunk | while | flops 2103305 | bytes 6352095 | solution.py:13
  300.3 0.7 dynamic_slice.82
  303.2 3.9 fusion.47
  307.2 0.7 dynamic_slice.82
  310.1 3.9 fusion.47
  314.0 0.7 dynamic_slice.82
  316.9 3.9 fusion.47
  320.8 0.7 dynamic_slice.82
  323.7 3.9 fusion.47
  327.6 0.7 dynamic_slice.82
  330.5 3.9 fusion.47
  337.4 3.9 fusion.47
  344.2 3.9 fusion.47
  351.0 3.9 fusion.47
  357.8 3.9 fusion.47
  364.6 3.9 fusion.47
  371.5 3.9 fusion.47
  378.3 3.9 fusion.47
  385.1 3.9 fusion.47
  389.0 0.7 dynamic_slice.82
  391.9 3.9 fusion.47
  395.8 0.7 dynamic_slice.82
  398.7 3.9 fusion.47
  402.7 1.6 dynamic-slice_multiply_fusion
  (95 shorter events, 8.0 us)
Async XLA Ops:
  7.2 51.5 %copy-start = (bf16[3,3,448,384]{3,2,1,0:T(8,128)(2,1)S(1)}, bf16[3,3,448,384]{3,2,1,0:T(8,128)(2,1)}, u32[]{:S(2)}) copy-start(bf16[3,3,448,384]{3,2,1,0:T(8,128)(2,1)} %param.24) | copy-start | bytes 9289732
  7.2 87.4 %all-gather.5.cloned.1.call-start = ((), (), s32[]{:S(2)}) async-start(), calls=%async_computation | async-start | bytes 1179648 | tf_op jit(solution)/shard_map/all_gather | solution.py:135
  7.2 5.7 %copy-start.2 = (bf16[16,17,17,768]{3,0,2,1:T(8,128)(2,1)S(1)}, bf16[16,17,17,768]{3,0,2,1:T(8,128)(2,1)}, u32[]{:S(2)}) copy-start(bf16[16,17,17,768]{3,0,2,1:T(8,128)(2,1)} %param.15) | copy-start | bytes 21307396
  7.2 5.7 %copy-start.11 = (bf16[1,1,768,384]{3,2,1,0:T(8,128)(2,1)S(1)}, bf16[1,1,768,384]{3,2,1,0:T(8,128)(2,1)}, u32[]{:S(2)}) copy-start(bf16[1,1,768,384]{3,2,1,0:T(8,128)(2,1)} %param.16) | copy-start | bytes 1769476
  12.9 4.1 %copy-start.5 = (bf16[3,3,192,320]{3,2,1,0:T(8,128)(2,1)S(1)}, bf16[3,3,192,320]{3,2,1,0:T(8,128)(2,1)}, u32[]{:S(2)}) copy-start(bf16[3,3,192,320]{3,2,1,0:T(8,128)(2,1)} %param.17) | copy-start | bytes 3317764
  17.1 3.0 copy-start.10
  46.5 6.3 %copy-start.1 = (bf16[16,8,8,1280]{3,0,2,1:T(8,128)(2,1)S(1)}, bf16[16,8,8,1280]{3,0,2,1:T(8,128)(2,1)}, u32[]{:S(2)}) copy-start(bf16[16,8,8,1280]{3,0,2,1:T(8,128)(2,1)} %concatenate.6) | copy-start | bytes 7864324
  46.5 6.3 %copy-start.4 = (f32[8,8]{1,0:T(8,128)S(1)}, f32[8,8]{1,0:T(8,128)}, u32[]{:S(2)}) copy-start(f32[8,8]{1,0:T(8,128)} %constant.112.clone.1) | copy-start | bytes 772
  52.9 1.6 copy-start.12
  54.5 1.2 copy-start.6
  55.6 1.5 copy-start.7
  58.7 4.6 %copy-start.8 = (bf16[3,1,384,384]{3,2,1,0:T(8,128)(2,1)S(1)}, bf16[3,1,384,384]{3,2,1,0:T(8,128)(2,1)}, u32[]{:S(2)}) copy-start(bf16[3,1,384,384]{3,2,1,0:T(8,128)(2,1)} %param.26) | copy-start | bytes 2654212
  63.3 1.5 copy-start.9
  67.3 230.0 %all-gather.7.cloned.1.call-start = ((), (), s32[]{:S(2)}) async-start(), calls=%async_computation.1 | async-start | bytes 35651584 | tf_op jit(solution)/shard_map/all_gather | solution.py:8
  97.2 3.2 copy-start.13
  402.7 1.6 copy-start.3
Sparse Core Ops, SparseCore 0:
  67.5 27.0 all-gather.4
  100.5 196.7 all-gather.6
where the time goes:
time: 412 us; the launch traced here: 411 us
  waiting for transfers between devices  171 us (42%)
  other arithmetic  70.5 us (17%)
  blocking collectives  52.1 us (13%)
  matrix products  49.3 us (12%)
  loops' own time  32.1 us (8%)
  local copies, waits for them, and re-layouts  22.1 us (5%)
  between operations  14.4 us (3%)
    all_gather x1, waiting for transfers between devices, combined_all(): gathered = jax.tree.map(lambda a: lax.all_gather(a, axis), part)  143 us
    add x15, other arithmetic, combine(): moment_a + moment_b  58.7 us
    conv_general_dilated x11, matrix products, rectify(): lax.conv_general_dilated(inputs, kernel, (stride, stride), padding, dimen...  46.2 us
    unnamed x1, blocking collectives  34.3 us
    another operation x1, loops' own time, combined_all(): lax.fori_loop(1, lax.axis_size(axis), lambda source, state: combine(state...  32.1 us
    all_gather x1, waiting for transfers between devices, local(): gathered = lax.all_gather(features, 'col', axis=0, tiled=True)  27.1 us
    all_gather x1, blocking collectives, combined_all(): gathered = jax.tree.map(lambda a: lax.all_gather(a, axis), part)  17.7 us
    dynamic_slice x32, local copies, waits for them, and re-layouts, take(): lax.dynamic_index_in_dim(a, source, 0, False)  13.2 us
  transfers between devices with their start and end apart: 2, of which 2 were waited for; matrix products, arithmetic and copies ran while one was open for 0% of the time, Pallas kernels for 0%

commit v1 on v0

v1 whole, which is shorter than its diff:
```python
import jax
import jax.numpy as jnp
from jax import lax
from jax.sharding import Mesh, PartitionSpec as P

AXES = ("y", "xh", "xl", "z", "core")
IMAGES = 2048
FEAT = 2048
LOCAL = 16
GROUP = 512


def rectify(inputs, kernel, stride, padding):
    result = lax.conv_general_dilated(
        inputs,
        kernel,
        (stride, stride),
        padding,
        dimension_numbers=("NHWC", "HWIO", "NHWC"),
        preferred_element_type=jnp.float32,
    )
    return jnp.maximum(result, 0.0).astype(jnp.bfloat16)


def spatial_mean(inputs):
    return jnp.mean(inputs.astype(jnp.float32), axis=(1, 2))


def network(
    block_inputs,
    first_entry,
    first_wide,
    first_row,
    first_column,
    first_reduce,
    second_entry,
    second_row,
    second_column,
    second_deep,
    deep_row,
    deep_column,
    pool_project,
):
    no_margin = ((0, 0), (0, 0))
    entry_out = rectify(block_inputs, first_entry, 1, no_margin)
    half_width = first_wide.shape[2]
    wide_out = rectify(entry_out[..., :half_width], first_wide, 2, no_margin)
    tower_out = rectify(entry_out[..., half_width:], first_row, 1, ((0, 0), (3, 3)))
    tower_out = rectify(tower_out, first_column, 1, ((3, 3), (0, 0)))
    tower_out = rectify(tower_out, first_reduce, 2, no_margin)
    maximum = lax.reduce_window(
        block_inputs,
        jnp.array(-jnp.inf, block_inputs.dtype),
        lax.max,
        (1, 3, 3, 1),
        (1, 2, 2, 1),
        "VALID",
    )
    middle = jnp.concatenate([wide_out, tower_out, maximum], axis=3)
    second = rectify(middle, second_entry, 1, no_margin)
    branch_width = second_row.shape[2]
    deep_width = second_deep.shape[2]
    plain_width = second_entry.shape[3] - branch_width - deep_width
    plain_out = second[..., :plain_width]
    branch_in = second[..., plain_width : plain_width + branch_width]
    deep_in = second[..., plain_width + branch_width :]
    row_a = rectify(branch_in, second_row, 1, ((0, 0), (1, 1)))
    col_a = rectify(branch_in, second_column, 1, ((1, 1), (0, 0)))
    deep_out = rectify(deep_in, second_deep, 1, ((1, 1), (1, 1)))
    row_b = rectify(deep_out, deep_row, 1, ((0, 0), (1, 1)))
    col_b = rectify(deep_out, deep_column, 1, ((1, 1), (0, 0)))
    pool_pad = ((0, 0), (1, 1), (1, 1), (0, 0))
    summed = lax.reduce_window(
        middle.astype(jnp.float32),
        jnp.array(0.0, jnp.float32),
        lax.add,
        (1, 3, 3, 1),
        (1, 1, 1, 1),
        pool_pad,
    )
    ones_map = jnp.ones((1, middle.shape[1], middle.shape[2], 1), jnp.float32)
    cell_count = lax.reduce_window(
        ones_map, jnp.array(0.0, jnp.float32), lax.add, (1, 3, 3, 1), (1, 1, 1, 1), pool_pad
    )
    averaged = (summed / cell_count).astype(jnp.bfloat16)
    pooled = rectify(averaged, pool_project, 1, no_margin)
    return jnp.concatenate(
        [
            spatial_mean(plain_out),
            spatial_mean(row_a),
            spatial_mean(col_a),
            spatial_mean(row_b),
            spatial_mean(col_b),
            spatial_mean(pooled),
        ],
        axis=1,
    )


def cut(array, index, size, axis):
    return lax.dynamic_slice_in_dim(array, index * size, size, axis)


def statistics(features):
    highest = lax.Precision.HIGHEST
    x = lax.axis_index("xh") * 2 + lax.axis_index("xl")
    core = lax.axis_index("core")
    row_block = lax.axis_index("y") * 4 + x
    col_block = lax.axis_index("z") * 2 + core
    rows = features.reshape(LOCAL, 4, 4, 128).transpose(2, 0, 1, 3).reshape(4, 1, LOCAL, 512)
    columns = features.reshape(LOCAL, 4, 512).transpose(1, 0, 2)[None]
    sums = jnp.sum(features, axis=0).reshape(1, 1, LOCAL, 128)
    message = jnp.concatenate(
        [
            jnp.broadcast_to(rows, (4, 4, LOCAL, 512)),
            jnp.broadcast_to(columns, (4, 4, LOCAL, 512)),
            jnp.broadcast_to(sums, (4, 4, LOCAL, 128)),
        ],
        axis=-1,
    ).reshape(16, LOCAL, 1152)
    got = lax.all_to_all(message, ("xh", "xl", "z"), 0, 0, tiled=True)
    half_sum = jnp.sum(got[:, :, 1024:], axis=0)
    other_columns = lax.dynamic_slice_in_dim(got, 512 + 256 * (1 - core), 256, 2)
    pass_on = jnp.concatenate([got[:, :, :512], other_columns], -1).reshape(256, 768)
    pass_on = jnp.concatenate(
        [pass_on, jnp.pad(half_sum, ((0, 0), (0, 640)))], 0
    )
    passed = lax.ppermute(pass_on, "core", [(0, 1), (1, 0)])
    group_mean = (half_sum + passed[256:, :128]).reshape(FEAT) / GROUP
    own_columns = lax.dynamic_slice_in_dim(got, 512 + 256 * core, 256, 2).reshape(256, 256)
    rows_mean = lax.dynamic_index_in_dim(group_mean.reshape(4, 4, 128), x, 1, False).reshape(512)
    centered_rows = (
        jnp.concatenate([got[:, :, :512].reshape(256, 512), passed[:256, :512]], 0) - rows_mean
    )
    centered_columns = jnp.concatenate([own_columns, passed[:256, 512:]], 0) - cut(
        group_mean, col_block, 256, 0
    )
    moments = jnp.einsum(
        "nf,nc->fc",
        centered_rows,
        centered_columns,
        precision=highest,
        preferred_element_type=jnp.float32,
    )
    parts = jnp.concatenate(
        [
            moments.reshape(4, 128, 256),
            jnp.broadcast_to(group_mean.reshape(1, 8, 256), (4, 8, 256)),
        ],
        axis=1,
    )
    parts = lax.all_to_all(parts, "y", 0, 0, tiled=True)
    means = parts[:, 128:].reshape(4, FEAT)
    feature_mean = jnp.sum(means, axis=0) / 4
    gap = means - feature_mean
    between = jnp.einsum(
        "gf,gc->fc",
        cut(gap, row_block, 128, 1),
        cut(gap, col_block, 256, 1),
        precision=highest,
        preferred_element_type=jnp.float32,
    )
    covariance = (jnp.sum(parts[:, :128], axis=0) + between * GROUP) / (IMAGES - 1)
    return feature_mean, covariance


def local(*arguments):
    return statistics(network(*arguments))


def solution(mesh):
    fine = Mesh(mesh.devices.reshape(4, 2, 2, 4, 2), AXES)
    placed = (P(AXES, None, None, None),) + (P(),) * 12
    return jax.shard_map(
        local,
        mesh=fine,
        in_specs=placed,
        out_specs=(P(), P(("y", "xh", "xl"), ("z", "core"))),
        check_vma=False,
    )
```

time: 412 us -> 123 us (0.30)
  waiting for transfers between devices: 171 us -> 28.8 us
  other arithmetic: 70.5 us -> 14 us
  blocking collectives: 52.1 us -> 0 us
  loops' own time: 32.1 us -> 0 us
  starting transfers between devices: 0.08 us -> 15.9 us
  between operations: 14.4 us -> 1.03 us
  local copies, waits for them, and re-layouts: 22.1 us -> 12.2 us
    all_gather x2 -> x0, waiting for transfers between devices: 171 us -> none  [the longest x1 143 us: combined_all(): gathered = jax.tree.map(lambda a: lax.all_gather(a, axis), part)]
    add x30 -> x0, other arithmetic: 58.9 us -> none  [the longest x15 58.7 us: combine(): moment_a + moment_b]
    unnamed x1 -> x0, blocking collectives: 34.3 us -> none
    another operation x1 -> x0, loops' own time: 32.1 us -> none  [combined_all(): lax.fori_loop(1, lax.axis_size(axis), lambda source, state: combine(state...]
    all_to_all x0 -> x2, waiting for transfers between devices: none -> 26.4 us  [the longest x1 17.1 us: statistics(): got = lax.all_to_all(message, ('xh', 'xl', 'z'), 0, 0, tiled=True)]
    all_gather x1 -> x0, blocking collectives: 17.7 us -> none  [combined_all(): gathered = jax.tree.map(lambda a: lax.all_gather(a, axis), part)]
    dynamic_slice x47 -> x3, local copies, waits for them, and re-layouts: 14.4 us -> 1.35 us  [the longest x1 1.26 us: statistics(): lax.dynamic_slice_in_dim(got, 512 + 256 * core, 256, 2).reshape(256, 256)]
    all_to_all x0 -> x2, starting transfers between devices: none -> 12.6 us  [the longest x1 8.46 us: statistics(): got = lax.all_to_all(message, ('xh', 'xl', 'z'), 0, 0, tiled=True)]
  transfers between devices with their start and end apart: 2 -> 3, of which waited for: 2 -> 3; matrix products, arithmetic and copies ran while one was open for 0% -> 0% of each run, Pallas kernels for 0% -> 0%
where the time goes in v1:
time: 123 us; the launch traced here: 122 us
  matrix products  49.9 us (41%)
  waiting for transfers between devices  28.8 us (23%)
  starting transfers between devices  15.9 us (13%)
  other arithmetic  14 us (11%)
  local copies, waits for them, and re-layouts  12.2 us (10%)
    conv_general_dilated x11, matrix products, rectify(): lax.conv_general_dilated(inputs, kernel, (stride, stride), padding, dimen...  46 us
    all_to_all x1, waiting for transfers between devices, statistics(): got = lax.all_to_all(message, ('xh', 'xl', 'z'), 0, 0, tiled=True)  17.1 us
    all_to_all x1, waiting for transfers between devices, statistics(): parts = lax.all_to_all(parts, 'y', 0, 0, tiled=True)  9.38 us
    all_to_all x1, starting transfers between devices, statistics(): got = lax.all_to_all(message, ('xh', 'xl', 'z'), 0, 0, tiled=True)  8.46 us
    another operation x1, other arithmetic, network(): lax.reduce_window(block_inputs, jnp.array(-jnp.inf, block_inputs.dtype),...  5.68 us
    concatenate x1, local copies, waits for them, and re-layouts, network(): middle = jnp.concatenate([wide_out, tower_out, maximum], axis=3)  5.38 us
    all_to_all x1, starting transfers between devices, statistics(): parts = lax.all_to_all(parts, 'y', 0, 0, tiled=True)  4.19 us
    ppermute x1, starting transfers between devices, statistics(): passed = lax.ppermute(pass_on, 'core', [(0, 1), (1, 0)])  3.26 us
  transfers between devices with their start and end apart: 3, of which 3 were waited for; matrix products, arithmetic and copies ran while one was open for 0% of the time, Pallas kernels for 0%

profile of v1, /device:TPU:1, one launch (start us, length us, event | category | flops | bytes accessed | tf_op | source)
XLA Modules:
  0.0 121.8 jit_solution(16059169830858013990)
XLA Ops:
  0.6 0.0 copy-start
  0.7 5.7 %fusion.36 = bf16[16,8,8,768]{3,0,2,1:T(8,128)(2,1)} fusion(bf16[16,17,17,768]{3,0,2,1:T(8,128)(2,1)} %param.13), kind=kOutput, calls=%fused_computation.73 | output fusion | flops 6291456 | bytes 8675328 | tf_op jit(solution)/shard_map/reduce_window | solution.py:51
  6.4 4.1 %maximum_convert_fusion = bf16[16,17,17,384]{3,0,2,1:T(8,128)(2,1)S(1)} fusion(bf16[16,17,17,768]{3,0,2,1:T(8,128)(2,1)S(1)} %copy-done.2, bf16[1,1,768,384]{3,2,1,0:T(8,128)(2,1)S(1)} %copy-done.12), kind=kOutput, calls=%fused_computation | convolution fusion | flops 2730897408 | bytes 11243520 | tf_op jit(solution)/shard_map/conv_general_dilated | solution.py:14
  10.5 11.7 %fusion.6 = bf16[16,17,17,192]{3,0,2,1:T(8,128)(2,1)} fusion(bf16[1,7,192,192]{3,2,1,0:T(8,128)(2,1)S(1)} %copy-done.11, bf16[16,17,17,384]{3,0,2,1:T(8,128)(2,1)S(1)} %maximum_convert_fusion), kind=kOutput, calls=%fused_computation.9 | convolution fusion | flops 2145779712 | bytes 4831232 | tf_op jit(solution)/shard_map/conv_general_dilated | solution.py:14
  22.2 3.0 %maximum_convert_fusion.11 = bf16[16,8,8,320]{3,0,2,1:T(8,128)(2,1)} fusion(bf16[3,3,192,320]{3,2,1,0:T(8,128)(2,1)S(1)} %copy-done.6, bf16[16,17,17,384]{3,0,2,1:T(8,128)(2,1)S(1)} %maximum_convert_fusion), kind=kOutput, calls=%fused_computation.24 | convolution fusion | flops 1133117440 | bytes 4349952 | tf_op jit(solution)/shard_map/conv_general_dilated | solution.py:14
  25.2 9.4 %fusion.13 = bf16[16,8,8,192]{3,0,2,1:T(8,128)(2,1)} fusion(bf16[3,3,192,192]{3,2,1,0:T(8,128)(2,1)} %param.18, bf16[7,1,192,192]{3,2,1,0:T(8,128)(2,1)} %param.17, bf16[16,17,17,192]{3,0,2,1:T(8,128)(2,1)} %fusion.6), kind=kOutput, calls=%fused_computation.27 | convolution fusion | flops 2830089216 | bytes 3348480 | tf_op jit(solution)/shard_map/conv_general_dilated | solution.py:14
  34.6 5.4 %concatenate.24 = bf16[16,8,8,1280]{3,0,2,1:T(8,128)(2,1)} concatenate(bf16[16,8,8,320]{3,0,2,1:T(8,128)(2,1)} %maximum_convert_fusion.11, bf16[16,8,8,192]{3,0,2,1:T(8,128)(2,1)} %fusion.13, bf16[16,8,8,768]{3,0,2,1:T(8,128)(2,1)} %fusion.36), dimensions={3} | concatenate | bytes 5242880 | tf_op jit(solution)/shard_map/concatenate | solution.py:59
  39.9 6.2 %fusion.4 = bf16[16,8,8,1152]{3,0,2,1:T(8,128)(2,1)S(1)} fusion(bf16[16,8,8,1280]{3,0,2,1:T(8,128)(2,1)} %concatenate.24, bf16[1,1,1280,1152]{3,2,1,0:T(8,128)(2,1)} %param.19), kind=kOutput, calls=%fused_computation.7 | convolution fusion | flops 3022258176 | bytes 7929856 | tf_op jit(solution)/shard_map/conv_general_dilated | solution.py:14
  46.1 0.2 convert_reduce_fusion.4
  46.3 0.0 copy-start.7
  46.3 4.6 %maximum_convert_fusion.8 = bf16[16,8,8,384]{3,0,2,1:T(8,128)(2,1)S(1)} fusion(bf16[3,3,448,384]{3,2,1,0:T(8,128)(2,1)S(1)} %copy-done, bf16[16,8,8,1152]{3,0,2,1:T(8,128)(2,1)S(1)} %fusion.4), kind=kOutput, calls=%fused_computation.18 | convolution fusion | flops 2665218048 | bytes 4931584 | tf_op jit(solution)/shard_map/conv_general_dilated | solution.py:14
  50.9 1.5 %convert_reduce_fusion = f32[16,384]{1,0:T(8,128)S(1)} fusion(bf16[16,8,8,384]{3,0,2,1:T(8,128)(2,1)S(1)} %maximum_convert_fusion.8, bf16[3,1,384,384]{3,2,1,0:T(8,128)(2,1)S(1)} %copy-done.7), kind=kOutput, calls=%fused_computation.14 | convolution fusion | flops 832038912 | bytes 1695744 | tf_op jit(solution)/shard_map/conv_general_dilated | solution.py:14
  52.4 1.5 %convert_reduce_fusion.1 = f32[16,384]{1,0:T(8,128)S(1)} fusion(bf16[16,8,8,384]{3,0,2,1:T(8,128)(2,1)S(1)} %maximum_convert_fusion.8, bf16[1,3,384,384]{3,2,1,0:T(8,128)(2,1)S(1)} %copy-done.8), kind=kOutput, calls=%fused_computation.16 | convolution fusion | flops 832038912 | bytes 1695744 | tf_op jit(solution)/shard_map/conv_general_dilated | solution.py:14
  53.9 1.5 %convert_reduce_fusion.2 = f32[16,384]{1,0:T(8,128)S(1)} fusion(bf16[3,1,384,384]{3,2,1,0:T(8,128)(2,1)S(1)} %copy-done.9, bf16[16,8,8,1152]{3,0,2,1:T(8,128)(2,1)S(1)} %fusion.4), kind=kOutput, calls=%fused_computation.19 | convolution fusion | flops 832038912 | bytes 1695744 | tf_op jit(solution)/shard_map/conv_general_dilated | solution.py:14
  55.4 0.0 copy-start.5
  55.4 1.5 %convert_reduce_fusion.3 = f32[16,384]{1,0:T(8,128)S(1)} fusion(bf16[1,3,384,384]{3,2,1,0:T(8,128)(2,1)S(1)} %copy-done.10, bf16[16,8,8,1152]{3,0,2,1:T(8,128)(2,1)S(1)} %fusion.4), kind=kOutput, calls=%fused_computation.21 | convolution fusion | flops 832038912 | bytes 1695744 | tf_op jit(solution)/shard_map/conv_general_dilated | solution.py:14
  57.0 0.2 copy-done.1
  57.1 1.6 %multiply_convert_fusion = bf16[16,8,8,1280]{3,0,2,1:T(8,128)(2,1)S(1)} fusion(bf16[16,8,8,1280]{3,0,2,1:T(8,128)(2,1)S(1)} %copy-done.1, f32[8,8]{1,0:T(8,128)S(1)} %copy-done.5), kind=kOutput, calls=%fused_computation.1 | output fusion | flops 14417920 | bytes 5243136 | tf_op jit(solution)/shard_map/reduce_window | solution.py:73
  58.7 1.2 fusion.16
  59.9 0.1 concatenate.25
  60.0 0.1 reshape.60
  60.1 0.7 reshape.61
  60.9 0.1 broadcast_in_dim.12
  61.0 1.0 copy.17
  62.0 0.1 broadcast_in_dim.13
  62.0 0.1 broadcast_in_dim.14
  62.1 1.2 pad_maximum_fusion
  63.3 8.5 %all-to-all-start = ((f32[16,16,1152]{2,1,0:T(8,128)}), f32[16,16,1152]{2,1,0:T(8,128)}, u32[]{:S(2)}, u32[]{:S(2)}) async-start(f32[16,16,1152]{2,1,0:T(8,128)} %bitcast.36), calls=%async_computation | async-start | bytes 2359296 | tf_op jit(solution)/shard_map/all_to_all | solution.py:121
  71.7 17.1 %all-to-all-done = f32[16,16,1152]{2,1,0:T(8,128)} async-done(((f32[16,16,1152]{2,1,0:T(8,128)}), f32[16,16,1152]{2,1,0:T(8,128)}, u32[]{:S(2)}, u32[]{:S(2)}) %all-to-all-start) | async-done | bytes 1179680 | tf_op jit(solution)/shard_map/all_to_all | solution.py:121
  88.8 1.1 slice.54
  89.9 1.3 %constant_dynamic-slice_fusion = (f32[16,16,256]{2,1,0:T(8,128)S(1)}, f32[16,16,256]{2,1,0:T(8,128)S(1)}) fusion(f32[16,16,1152]{2,1,0:T(8,128)} %all-to-all-done, s32[]{:T(128)S(6)} %select_n.19, s32[]{:T(128)S(6)} %select_n.17), kind=kLoop, calls=%fused_computation.68 | loop fusion | bytes 1048584 | tf_op jit(solution)/shard_map/dynamic_slice | solution.py:130
  91.2 0.1 pad_maximum_fusion.1
  91.2 0.9 slice_reduce_fusion.1
  92.2 1.0 select_maximum_fusion
  93.1 3.3 %collective-permute-start = (f32[272,768]{1,0:T(8,128)}, f32[272,768]{1,0:T(8,128)}, u32[]{:S(2)}, u32[]{:S(2)}) collective-permute-start(f32[272,768]{1,0:T(8,128)} %select_maximum_fusion), channel_id=1, source_target_pairs={{0,1},{1,0},{2,3},{3,2},{4,5},{5,4},{6,7},{7,6},{8,9},{9,8},{10,11... | collective-permute-start | bytes 2506760 | tf_op jit(solution)/shard_map/ppermute | solution.py:128
  96.4 2.3 %collective-permute-done = f32[272,768]{1,0:T(8,128)} collective-permute-done((f32[272,768]{1,0:T(8,128)}, f32[272,768]{1,0:T(8,128)}, u32[]{:S(2)}, u32[]{:S(2)}) %collective-permute-start) | collective-permute-done | bytes 835616 | tf_op jit(solution)/shard_map/ppermute | solution.py:128
  98.7 0.7 fusion.29
  99.4 0.1 dynamic_slice.22
  99.5 1.1 slice.56
  100.6 1.0 slice.58
  101.5 2.9 %fusion.20 = f32[512,256]{1,0:T(8,128)S(1)} fusion(f32[256,512]{1,0:T(8,128)S(1)} %slice.56, f32[256,512]{1,0:T(8,128)} %bitcast.35, f32[256,256]{1,0:T(8,128)S(1)} %slice.58, f32[256,256]{1,0:T(8,128)S(1)} %bitcast.39, f32[512]{0:T(512)S(1)} %bitcast.48, f32[256]{0:T(256)S(1)} %dynamic_slice.22), kind=kOutput, calls=%fused_computation.37 | convolution fusion | flops 806092800 | bytes 2100224 | tf_op jit(solution)/shard_map/nf,nc->fc/dot_general | solution.py:138
  104.4 0.8 pad_maximum_fusion.2
  105.3 4.2 %all-to-all-start.1 = ((f32[4,136,256]{2,1,0:T(8,128)}), f32[4,136,256]{2,1,0:T(8,128)}, u32[]{:S(2)}, u32[]{:S(2)}) async-start(f32[4,136,256]{2,1,0:T(8,128)} %pad_maximum_fusion.2), calls=%async_computation.1 | async-start | bytes 1114112 | tf_op jit(solution)/shard_map/all_to_all | solution.py:152
  109.5 9.4 %all-to-all-done.1 = f32[4,136,256]{2,1,0:T(8,128)} async-done(((f32[4,136,256]{2,1,0:T(8,128)}), f32[4,136,256]{2,1,0:T(8,128)}, u32[]{:S(2)}, u32[]{:S(2)}) %all-to-all-start.1) | async-done | bytes 557088 | tf_op jit(solution)/shard_map/all_to_all | solution.py:152
  118.8 0.8 slice_bitcast_fusion
  119.6 0.0 copy-start.4
  119.7 1.1 slice_reduce_fusion
  120.8 1.0 fusion.18
  (37 shorter events, 0.2 us)
Async XLA Ops:
  0.6 45.7 %copy-start = (bf16[3,3,448,384]{3,2,1,0:T(8,128)(2,1)S(1)}, bf16[3,3,448,384]{3,2,1,0:T(8,128)(2,1)}, u32[]{:S(2)}) copy-start(bf16[3,3,448,384]{3,2,1,0:T(8,128)(2,1)} %param.22) | copy-start | bytes 9289732
  0.6 5.7 %copy-start.2 = (bf16[16,17,17,768]{3,0,2,1:T(8,128)(2,1)S(1)}, bf16[16,17,17,768]{3,0,2,1:T(8,128)(2,1)}, u32[]{:S(2)}) copy-start(bf16[16,17,17,768]{3,0,2,1:T(8,128)(2,1)} %param.13) | copy-start | bytes 21307396
  0.7 5.7 %copy-start.12 = (bf16[1,1,768,384]{3,2,1,0:T(8,128)(2,1)S(1)}, bf16[1,1,768,384]{3,2,1,0:T(8,128)(2,1)}, u32[]{:S(2)}) copy-start(bf16[1,1,768,384]{3,2,1,0:T(8,128)(2,1)} %param.14) | copy-start | bytes 1769476
  6.4 4.1 %copy-start.11 = (bf16[1,7,192,192]{3,2,1,0:T(8,128)(2,1)S(1)}, bf16[1,7,192,192]{3,2,1,0:T(8,128)(2,1)}, u32[]{:S(2)}) copy-start(bf16[1,7,192,192]{3,2,1,0:T(8,128)(2,1)} %param.16) | copy-start | bytes 1548292
  10.5 11.7 %copy-start.6 = (bf16[3,3,192,320]{3,2,1,0:T(8,128)(2,1)S(1)}, bf16[3,3,192,320]{3,2,1,0:T(8,128)(2,1)}, u32[]{:S(2)}) copy-start(bf16[3,3,192,320]{3,2,1,0:T(8,128)(2,1)} %param.15) | copy-start | bytes 3317764
  46.3 4.6 %copy-start.7 = (bf16[3,1,384,384]{3,2,1,0:T(8,128)(2,1)S(1)}, bf16[3,1,384,384]{3,2,1,0:T(8,128)(2,1)}, u32[]{:S(2)}) copy-start(bf16[3,1,384,384]{3,2,1,0:T(8,128)(2,1)} %param.24) | copy-start | bytes 2654212
  50.9 1.5 %copy-start.8 = (bf16[1,3,384,384]{3,2,1,0:T(8,128)(2,1)S(1)}, bf16[1,3,384,384]{3,2,1,0:T(8,128)(2,1)}, u32[]{:S(2)}) copy-start(bf16[1,3,384,384]{3,2,1,0:T(8,128)(2,1)} %param.23) | copy-start | bytes 2654212
  52.4 1.5 %copy-start.9 = (bf16[3,1,384,384]{3,2,1,0:T(8,128)(2,1)S(1)}, bf16[3,1,384,384]{3,2,1,0:T(8,128)(2,1)}, u32[]{:S(2)}) copy-start(bf16[3,1,384,384]{3,2,1,0:T(8,128)(2,1)} %param.21) | copy-start | bytes 2654212
  53.9 1.5 %copy-start.10 = (bf16[1,3,384,384]{3,2,1,0:T(8,128)(2,1)S(1)}, bf16[1,3,384,384]{3,2,1,0:T(8,128)(2,1)}, u32[]{:S(2)}) copy-start(bf16[1,3,384,384]{3,2,1,0:T(8,128)(2,1)} %param.20) | copy-start | bytes 2654212
  55.4 1.7 %copy-start.1 = (bf16[16,8,8,1280]{3,0,2,1:T(8,128)(2,1)S(1)}, bf16[16,8,8,1280]{3,0,2,1:T(8,128)(2,1)}, u32[]{:S(2)}) copy-start(bf16[16,8,8,1280]{3,0,2,1:T(8,128)(2,1)} %concatenate.24) | copy-start | bytes 7864324
  55.4 1.7 %copy-start.5 = (f32[8,8]{1,0:T(8,128)S(1)}, f32[8,8]{1,0:T(8,128)}, u32[]{:S(2)}) copy-start(f32[8,8]{1,0:T(8,128)} %constant.29.clone.1) | copy-start | bytes 772
  57.1 1.6 %copy-start.13 = (bf16[1,1,1280,192]{2,3,1,0:T(8,128)(2,1)S(1)}, bf16[1,1,1280,192]{2,3,1,0:T(8,128)(2,1)}, u32[]{:S(2)}) copy-start(bf16[1,1,1280,192]{2,3,1,0:T(8,128)(2,1)} %param.25) | copy-start | bytes 1474564
  63.3 25.5 %all-to-all-start = ((f32[16,16,1152]{2,1,0:T(8,128)}), f32[16,16,1152]{2,1,0:T(8,128)}, u32[]{:S(2)}, u32[]{:S(2)}) async-start(f32[16,16,1152]{2,1,0:T(8,128)} %bitcast.36), calls=%async_computation | async-start | bytes 2359296 | tf_op jit(solution)/shard_map/all_to_all | solution.py:121
  89.9 1.3 %copy-start.3 = (f32[16,16,512]{2,1,0:T(8,128)}, f32[16,16,512]{2,1,0:T(8,128)S(1)}, u32[]{:S(2)}) copy-start(f32[16,16,512]{2,1,0:T(8,128)S(1)} %slice.54) | copy-start | bytes 1572868
  93.1 5.6 %collective-permute-start = (f32[272,768]{1,0:T(8,128)}, f32[272,768]{1,0:T(8,128)}, u32[]{:S(2)}, u32[]{:S(2)}) collective-permute-start(f32[272,768]{1,0:T(8,128)} %select_maximum_fusion), channel_id=1, source_target_pairs={{0,1},{1,0},{2,3},{3,2},{4,5},{5,4},{6,7},{7,6},{8,9},{9,8},{10,11... | collective-permute-start | bytes 2506760 | tf_op jit(solution)/shard_map/ppermute | solution.py:128
  105.3 13.6 %all-to-all-start.1 = ((f32[4,136,256]{2,1,0:T(8,128)}), f32[4,136,256]{2,1,0:T(8,128)}, u32[]{:S(2)}, u32[]{:S(2)}) async-start(f32[4,136,256]{2,1,0:T(8,128)} %pad_maximum_fusion.2), calls=%async_computation.1 | async-start | bytes 1114112 | tf_op jit(solution)/shard_map/all_to_all | solution.py:152
  119.6 2.1 %copy-start.4 = (f32[1,2,8,128]{3,1,2,0:T(2,128)}, f32[1,2,8,128]{3,1,2,0:T(2,128)S(1)}, u32[]{:S(2)}) copy-start(f32[1,2,8,128]{3,1,2,0:T(2,128)S(1)} %copy.18) | copy-start | bytes 24580

commit v2 on v1

v2 whole, which is shorter than its diff:
```python
import jax
import jax.numpy as jnp
from jax import lax
from jax.experimental import pallas as pl
from jax.experimental.pallas import tpu as pltpu
from jax.sharding import Mesh, PartitionSpec as P

AXES = ("y", "xh", "xl", "z", "core")
IMAGES = 2048
FEAT = 2048
LOCAL = 16
GROUP = 512


BF = jnp.bfloat16
F32 = jnp.float32


def relu(values):
    return jnp.maximum(values, 0.0).astype(BF)


def dot(a, b):
    return jnp.dot(a, b, preferred_element_type=F32)


def place_sum(values):
    return jnp.sum(values.astype(F32).reshape(64, LOCAL, -1), axis=0) * (1.0 / 64.0)


def network_kernel(
    x_hbm,
    entry_hbm,
    wide_hbm,
    row_hbm,
    column_hbm,
    reduce_hbm,
    second_hbm,
    second_row_hbm,
    second_column_hbm,
    second_deep_hbm,
    deep_row_hbm,
    deep_column_hbm,
    pool_hbm,
    out,
    x,
    entry_w,
    wide_w,
    row_w,
    column_w,
    reduce_w,
    second_w,
    second_row_w,
    second_column_w,
    second_deep_w,
    deep_row_w,
    deep_column_w,
    pool_w,
    row_pad,
    short,
    long,
    row_out,
    tower,
    middle,
    branch,
    deep,
    deep_out,
    averaged,
    features,
    sems,
):
    copies = {}

    def start(name, source, target, slot):
        copies[name] = pltpu.make_async_copy(source, target, sems.at[slot])
        copies[name].start()

    start("entry", entry_hbm, entry_w, 0)
    start("x0", x_hbm.at[pl.ds(0, 9)], x.at[pl.ds(0, 9)], 1)
    start("x1", x_hbm.at[pl.ds(9, 8)], x.at[pl.ds(9, 8)], 2)
    later = [
        ("row", row_hbm, row_w),
        ("column", column_hbm, column_w),
        ("wide", wide_hbm, wide_w),
        ("reduce", reduce_hbm, reduce_w),
        ("second", second_hbm, second_w),
        ("second_deep", second_deep_hbm, second_deep_w),
        ("second_row", second_row_hbm, second_row_w),
        ("second_column", second_column_hbm, second_column_w),
        ("deep_row", deep_row_hbm, deep_row_w),
        ("deep_column", deep_column_hbm, deep_column_w),
        ("pool", pool_hbm, pool_w),
    ]
    for i, (name, source, target) in enumerate(later):
        start(name, source, target, 3 + i)

    long[:, 0:3] = jnp.zeros((17, 3, LOCAL, 256), BF)
    long[:, 20:23] = jnp.zeros((17, 3, LOCAL, 256), BF)
    row_out[0:3] = jnp.zeros((3, 17, LOCAL, 192), BF)
    row_out[20:23] = jnp.zeros((3, 17, LOCAL, 192), BF)
    row_pad[:, 0:64] = jnp.zeros((7, 64, 192), BF)
    for array, channels in ((middle, 1280), (branch, 384), (deep, 448), (deep_out, 384)):
        array[0] = jnp.zeros((10, LOCAL, channels), BF)
        array[9] = jnp.zeros((10, LOCAL, channels), BF)
        array[1:9, 0] = jnp.zeros((8, LOCAL, channels), BF)
        array[1:9, 9] = jnp.zeros((8, LOCAL, channels), BF)

    copies["entry"].wait()
    copies["x0"].wait()

    def entry_block(i, carry):
        @pl.when(i == 1)
        def _():
            copies["x1"].wait()

        values = relu(dot(x[pl.ds(8 * i, 9)].reshape(2448, 768), entry_w[...]))
        values = values.reshape(9, 17, LOCAL, 384)
        long[pl.ds(8 * i, 9), 3:20] = values[..., 128:]
        for r in range(9):
            for c in range(17):
                short[r % 2, c % 2, 4 * i + r // 2, c // 2] = values[r, c, :, :192]
        return carry

    lax.fori_loop(0, 2, entry_block, 0)

    copies["row"].wait()
    row_pad[:, 64:] = row_w[...]

    def row_block(i, carry):
        values = sum(
            dot(long[pl.ds(8 * i, 9), t : t + 17].reshape(2448, 256), row_pad[t])
            for t in range(7)
        )
        row_out[pl.ds(8 * i + 3, 9)] = relu(values).reshape(9, 17, LOCAL, 192)
        for r in range(4):
            tall = jnp.maximum(
                jnp.maximum(x[8 * i + 2 * r], x[8 * i + 2 * r + 1]), x[8 * i + 2 * r + 2]
            )
            for c in range(8):
                middle[4 * i + r + 1, c + 1, :, 512:] = jnp.maximum(
                    jnp.maximum(tall[2 * c], tall[2 * c + 1]), tall[2 * c + 2]
                )
        return carry

    lax.fori_loop(0, 2, row_block, 0)
    copies["column"].wait()

    def column_block(i, carry):
        values = sum(
            dot(row_out[pl.ds(8 * i + t, 9)].reshape(2448, 192), column_w[t]) for t in range(7)
        )
        values = relu(values).reshape(9, 17, LOCAL, 192)
        for r in range(9):
            for c in range(17):
                tower[r % 2, c % 2, 4 * i + r // 2, c // 2] = values[r, c]
        return carry

    lax.fori_loop(0, 2, column_block, 0)
    copies["wide"].wait()
    copies["reduce"].wait()

    def strided(array, weights):
        return sum(
            dot(
                array[a % 2, b % 2, a // 2 : a // 2 + 8, b // 2 : b // 2 + 8].reshape(1024, 192),
                weights[a, b],
            )
            for a in range(3)
            for b in range(3)
        )

    wide_out = relu(strided(short, wide_w))
    middle[1:9, 1:9, :, 0:320] = wide_out.reshape(8, 8, LOCAL, 320)
    tower_out = relu(strided(tower, reduce_w))
    middle[1:9, 1:9, :, 320:512] = tower_out.reshape(8, 8, LOCAL, 192)

    copies["second"].wait()
    flat = middle[1:9, 1:9].reshape(1024, 1280)
    second = relu(dot(flat, second_w[...]))
    features[:, 0:320] = place_sum(second[:, 0:320])
    branch[1:9, 1:9] = second[:, 320:704].reshape(8, 8, LOCAL, 384)
    deep[1:9, 1:9] = second[:, 704:1152].reshape(8, 8, LOCAL, 448)

    def window(array, a, b):
        return array[a : a + 8, b : b + 8].reshape(1024, array.shape[3])

    def across(array, weights):
        taps = jnp.concatenate([window(array, 1, t) for t in range(3)], axis=1)
        return relu(dot(taps, weights[...].reshape(1152, 384)))

    def down(array, weights):
        taps = jnp.concatenate([window(array, t, 1) for t in range(3)], axis=1)
        return relu(dot(taps, weights[...].reshape(1152, 384)))

    copies["second_deep"].wait()
    deep_values = sum(
        dot(window(deep, a, b), second_deep_w[a, b]) for a in range(3) for b in range(3)
    )
    deep_out[1:9, 1:9] = relu(deep_values).reshape(8, 8, LOCAL, 384)

    for i in range(8):
        tall = (
            middle[i].astype(F32) + middle[i + 1].astype(F32) + middle[i + 2].astype(F32)
        )
        rows_inside = 3 - (i == 0) - (i == 7)
        for j in range(8):
            cells = rows_inside * (3 - (j == 0) - (j == 7))
            box = (tall[j] + tall[j + 1] + tall[j + 2]) * (1.0 / cells)
            averaged[i, j] = box.astype(BF)

    copies["second_row"].wait()
    features[:, 320:704] = place_sum(across(branch, second_row_w))
    copies["second_column"].wait()
    features[:, 704:1088] = place_sum(down(branch, second_column_w))
    copies["deep_row"].wait()
    features[:, 1088:1472] = place_sum(across(deep_out, deep_row_w))
    copies["deep_column"].wait()
    features[:, 1472:1856] = place_sum(down(deep_out, deep_column_w))
    copies["pool"].wait()
    pooled = lax.dot_general(
        averaged[...].reshape(1024, 1280),
        pool_w[...],
        (((1,), (1,)), ((), ())),
        preferred_element_type=F32,
    )
    features[:, 1856:2048] = place_sum(relu(pooled))

    for block in range(16):
        part = features[:, 128 * block : 128 * block + 128]
        total = jnp.sum(part, axis=0, keepdims=True)
        for target in range(16):
            target_x, target_z = target // 4, target % 4
            if block % 4 == target_x:
                out[target, :, 128 * (block // 4) : 128 * (block // 4) + 128] = part
            if block // 4 == target_z:
                out[target, :, 512 + 128 * (block % 4) : 640 + 128 * (block % 4)] = part
            out[target, block : block + 1, 1024:1152] = total


def network(
    block_inputs,
    first_entry,
    first_wide,
    first_row,
    first_column,
    first_reduce,
    second_entry,
    second_row,
    second_column,
    second_deep,
    deep_row,
    deep_column,
    pool_project,
):
    operands = (
        block_inputs.transpose(1, 2, 0, 3),
        first_entry[0, 0],
        first_wide,
        first_row[0],
        first_column[:, 0],
        first_reduce,
        second_entry[0, 0],
        second_row[0],
        second_column[:, 0],
        second_deep,
        deep_row[0],
        deep_column[:, 0],
        pool_project[0, 0].T,
    )
    place = lambda *shape: pltpu.VMEM(shape, BF)
    return pl.pallas_call(
        network_kernel,
        out_shape=jax.ShapeDtypeStruct((16, LOCAL, 1152), F32),
        in_specs=[pl.BlockSpec(memory_space=pl.ANY)] * 13,
        out_specs=pl.BlockSpec(memory_space=pltpu.VMEM),
        scratch_shapes=[pltpu.VMEM(a.shape, a.dtype) for a in operands]
        + [
            place(7, 256, 192),
            place(2, 2, 9, 9, LOCAL, 192),
            place(17, 23, LOCAL, 256),
            place(23, 17, LOCAL, 192),
            place(2, 2, 9, 9, LOCAL, 192),
            place(10, 10, LOCAL, 1280),
            place(10, 10, LOCAL, 384),
            place(10, 10, LOCAL, 448),
            place(10, 10, LOCAL, 384),
            place(8, 8, LOCAL, 1280),
            pltpu.VMEM((LOCAL, 2048), F32),
            pltpu.SemaphoreType.DMA((14,)),
        ],
        compiler_params=pltpu.CompilerParams(vmem_limit_bytes=67043328),
        cost_estimate=pl.CostEstimate(
            flops=19600000000, bytes_accessed=21000000, transcendentals=0
        ),
        name="network",
    )(*operands)


def cut(array, index, size, axis):
    return lax.dynamic_slice_in_dim(array, index * size, size, axis)


def statistics(message):
    highest = lax.Precision.HIGHEST
    x = lax.axis_index("xh") * 2 + lax.axis_index("xl")
    core = lax.axis_index("core")
    row_block = lax.axis_index("y") * 4 + x
    col_block = lax.axis_index("z") * 2 + core
    got = lax.all_to_all(message, ("xh", "xl", "z"), 0, 0, tiled=True)
    half_sum = jnp.sum(got[:, :, 1024:], axis=0)
    other_columns = lax.dynamic_slice_in_dim(got, 512 + 256 * (1 - core), 256, 2)
    pass_on = jnp.concatenate([got[:, :, :512], other_columns], -1).reshape(256, 768)
    pass_on = jnp.concatenate(
        [pass_on, jnp.pad(half_sum, ((0, 0), (0, 640)))], 0
    )
    passed = lax.ppermute(pass_on, "core", [(0, 1), (1, 0)])
    group_mean = (half_sum + passed[256:, :128]).reshape(FEAT) / GROUP
    own_columns = lax.dynamic_slice_in_dim(got, 512 + 256 * core, 256, 2).reshape(256, 256)
    rows_mean = lax.dynamic_index_in_dim(group_mean.reshape(4, 4, 128), x, 1, False).reshape(512)
    centered_rows = (
        jnp.concatenate([got[:, :, :512].reshape(256, 512), passed[:256, :512]], 0) - rows_mean
    )
    centered_columns = jnp.concatenate([own_columns, passed[:256, 512:]], 0) - cut(
        group_mean, col_block, 256, 0
    )
    moments = jnp.einsum(
        "nf,nc->fc",
        centered_rows,
        centered_columns,
        precision=highest,
        preferred_element_type=jnp.float32,
    )
    parts = jnp.concatenate(
        [
            moments.reshape(4, 128, 256),
            jnp.broadcast_to(group_mean.reshape(1, 8, 256), (4, 8, 256)),
        ],
        axis=1,
    )
    parts = lax.all_to_all(parts, "y", 0, 0, tiled=True)
    means = parts[:, 128:].reshape(4, FEAT)
    feature_mean = jnp.sum(means, axis=0) / 4
    gap = means - feature_mean
    between = jnp.einsum(
        "gf,gc->fc",
        cut(gap, row_block, 128, 1),
        cut(gap, col_block, 256, 1),
        precision=highest,
        preferred_element_type=jnp.float32,
    )
    covariance = (jnp.sum(parts[:, :128], axis=0) + between * GROUP) / (IMAGES - 1)
    return feature_mean, covariance


def local(*arguments):
    return statistics(network(*arguments))


def solution(mesh):
    fine = Mesh(mesh.devices.reshape(4, 2, 2, 4, 2), AXES)
    placed = (P(AXES, None, None, None),) + (P(),) * 12
    return jax.shard_map(
        local,
        mesh=fine,
        in_specs=placed,
        out_specs=(P(), P(("y", "xh", "xl"), ("z", "core"))),
        check_vma=False,
    )
```

time: 123 us -> 100 us (0.81)
  Pallas kernels: 0 us -> 50.7 us
  matrix products: 49.9 us -> 2.82 us
  other arithmetic: 14 us -> 1.04 us
  local copies, waits for them, and re-layouts: 12.2 us -> 0.32 us
    pallas_call x0 -> x1, Pallas kernels: none -> 50.7 us  [network(): pl.pallas_call(network_kernel, out_shape=jax.ShapeDtypeStruct((16, LOCAL,...]
    conv_general_dilated x11 -> x0, matrix products: 46 us -> none  [rectify(): lax.conv_general_dilated(inputs, kernel, (stride, stride), padding, dimen...]
    another operation x2 -> x0, other arithmetic: 7.24 us -> none  [the longest x1 5.68 us: network(): lax.reduce_window(block_inputs, jnp.array(-jnp.inf, block_inputs.dtype),...]
    concatenate x2 -> x0, local copies, waits for them, and re-layouts: 5.49 us -> none  [the longest x1 5.38 us: network(): middle = jnp.concatenate([wide_out, tower_out, maximum], axis=3)]
where the time goes in v2:
time: 100 us; the launch traced here: 99.8 us
  Pallas kernels  50.7 us (51%)
  waiting for transfers between devices  28.2 us (28%)
  starting transfers between devices  15.9 us (16%)
  matrix products  2.82 us (3%)
  other arithmetic  1.04 us (1%)
    pallas_call x1, Pallas kernels, network(): pl.pallas_call(network_kernel, out_shape=jax.ShapeDtypeStruct((16, LOCAL,...  50.7 us
    all_to_all x1, waiting for transfers between devices, statistics(): got = lax.all_to_all(message, ('xh', 'xl', 'z'), 0, 0, tiled=True)  17 us
    all_to_all x1, waiting for transfers between devices, statistics(): parts = lax.all_to_all(parts, 'y', 0, 0, tiled=True)  9.26 us
    all_to_all x1, starting transfers between devices, statistics(): got = lax.all_to_all(message, ('xh', 'xl', 'z'), 0, 0, tiled=True)  8.41 us
    all_to_all x1, starting transfers between devices, statistics(): parts = lax.all_to_all(parts, 'y', 0, 0, tiled=True)  4.19 us
    ppermute x1, starting transfers between devices, statistics(): passed = lax.ppermute(pass_on, 'core', [(0, 1), (1, 0)])  3.34 us
  transfers between devices with their start and end apart: 3, of which 3 were waited for; matrix products, arithmetic and copies ran while one was open for 0% of the time, Pallas kernels for 0%

profile of v2, /device:TPU:1, one launch (start us, length us, event | category | flops | bytes accessed | tf_op | source)
XLA Modules:
  0.0 99.8 jit_solution(2250944584266411088)
XLA Ops:
  0.6 50.7 %network.1 = f32[16,16,1152]{2,1,0:T(8,128)} custom-call(bf16[17,17,16,768]{3,2,1,0:T(8,128)(2,1)} %bitcast.35, bf16[768,384]{1,0:T(8,128)(2,1)} %bitcast.43, bf16[3,3,192,320]{3,2,1,0:T(8,128)(2,1)} %wide_hbm.1, bf16[7,192,192]{2,1,0:T(8,128)(2,1)} %bitcast.41, bf16[7,192,192]{2,1,0:T(8,128)(2,1)} %bitcast.42, bf16[3,3,192,192]{3,2,1,0:T(8,128)(2,1)} %reduce_hbm.1, ...), custom_call_target="tpu_custom_call" | custom-call | flops 19599998976 | bytes 21000000 | tf_op jit(solution)/shard_map/network/pallas_call | solution.py:271
  51.3 8.4 %all-to-all-start = ((f32[16,16,1152]{2,1,0:T(8,128)}), f32[16,16,1152]{2,1,0:T(8,128)S(1)}, u32[]{:S(2)}, u32[]{:S(2)}) async-start(f32[16,16,1152]{2,1,0:T(8,128)} %network.1), calls=%async_computation | async-start | bytes 2359296 | tf_op jit(solution)/shard_map/all_to_all | solution.py:309
  59.8 17.0 %all-to-all-done = f32[16,16,1152]{2,1,0:T(8,128)S(1)} async-done(((f32[16,16,1152]{2,1,0:T(8,128)}), f32[16,16,1152]{2,1,0:T(8,128)S(1)}, u32[]{:S(2)}, u32[]{:S(2)}) %all-to-all-start) | async-done | bytes 1179680 | tf_op jit(solution)/shard_map/all_to_all | solution.py:309
  76.8 0.1 constant_dynamic-slice_fusion
  76.9 0.1 pad_maximum_fusion
  77.0 0.1 select_maximum_fusion
  77.1 3.3 %collective-permute-start = (f32[272,768]{1,0:T(8,128)S(1)}, f32[272,768]{1,0:T(8,128)S(1)}, u32[]{:S(2)}, u32[]{:S(2)}) collective-permute-start(f32[272,768]{1,0:T(8,128)S(1)} %select_maximum_fusion), channel_id=1, source_target_pairs={{0,1},{1,0},{2,3},{3,2},{4,5},{5,4},{6,7},{7,6},{8,9},{9,8},{10,11... | collective-permute-start | bytes 2506760 | tf_op jit(solution)/shard_map/ppermute | solution.py:316
  80.4 2.0 %collective-permute-done = f32[272,768]{1,0:T(8,128)S(1)} collective-permute-done((f32[272,768]{1,0:T(8,128)S(1)}, f32[272,768]{1,0:T(8,128)S(1)}, u32[]{:S(2)}, u32[]{:S(2)}) %collective-permute-start) | collective-permute-done | bytes 835616 | tf_op jit(solution)/shard_map/ppermute | solution.py:316
  82.4 0.1 dynamic_slice.22
  82.5 0.1 slice.31
  82.6 1.8 %fusion.2 = f32[512,256]{1,0:T(8,128)S(1)} fusion(f32[256,512]{1,0:T(8,128)S(1)} %slice.31, f32[256,512]{1,0:T(8,128)S(1)} %bitcast.25, f32[256,256]{1,0:T(8,128)S(1)} %slice.33, f32[256,256]{1,0:T(8,128)S(1)} %bitcast.28, f32[512]{0:T(512)S(1)} %bitcast.34, f32[256]{0:T(256)S(1)} %dynamic_slice.22), kind=kOutput, calls=%fused_computation.4 | convolution fusion | flops 806092800 | bytes 2100224 | tf_op jit(solution)/shard_map/nf,nc->fc/dot_general | solution.py:326
  84.4 0.8 pad_maximum_fusion.1
  85.3 4.2 %all-to-all-start.1 = ((f32[4,136,256]{2,1,0:T(8,128)}), f32[4,136,256]{2,1,0:T(8,128)S(1)}, u32[]{:S(2)}, u32[]{:S(2)}) async-start(f32[4,136,256]{2,1,0:T(8,128)} %pad_maximum_fusion.1), calls=%async_computation.1 | async-start | bytes 1114112 | tf_op jit(solution)/shard_map/all_to_all | solution.py:340
  89.4 9.3 %all-to-all-done.1 = f32[4,136,256]{2,1,0:T(8,128)S(1)} async-done(((f32[4,136,256]{2,1,0:T(8,128)}), f32[4,136,256]{2,1,0:T(8,128)S(1)}, u32[]{:S(2)}, u32[]{:S(2)}) %all-to-all-start.1) | async-done | bytes 557088 | tf_op jit(solution)/shard_map/all_to_all | solution.py:340
  98.7 0.0 copy-start
  98.8 1.0 fusion.1
  99.8 0.0 copy-done
  (13 shorter events, 0.2 us)
Async XLA Ops:
  51.3 25.4 %all-to-all-start = ((f32[16,16,1152]{2,1,0:T(8,128)}), f32[16,16,1152]{2,1,0:T(8,128)S(1)}, u32[]{:S(2)}, u32[]{:S(2)}) async-start(f32[16,16,1152]{2,1,0:T(8,128)} %network.1), calls=%async_computation | async-start | bytes 2359296 | tf_op jit(solution)/shard_map/all_to_all | solution.py:309
  77.1 5.3 %collective-permute-start = (f32[272,768]{1,0:T(8,128)S(1)}, f32[272,768]{1,0:T(8,128)S(1)}, u32[]{:S(2)}, u32[]{:S(2)}) collective-permute-start(f32[272,768]{1,0:T(8,128)S(1)} %select_maximum_fusion), channel_id=1, source_target_pairs={{0,1},{1,0},{2,3},{3,2},{4,5},{5,4},{6,7},{7,6},{8,9},{9,8},{10,11... | collective-permute-start | bytes 2506760 | tf_op jit(solution)/shard_map/ppermute | solution.py:316
  85.3 13.4 %all-to-all-start.1 = ((f32[4,136,256]{2,1,0:T(8,128)}), f32[4,136,256]{2,1,0:T(8,128)S(1)}, u32[]{:S(2)}, u32[]{:S(2)}) async-start(f32[4,136,256]{2,1,0:T(8,128)} %pad_maximum_fusion.1), calls=%async_computation.1 | async-start | bytes 1114112 | tf_op jit(solution)/shard_map/all_to_all | solution.py:340
  98.7 1.1 %copy-start = (f32[1,2,8,128]{3,1,2,0:T(2,128)}, f32[1,2,8,128]{3,1,2,0:T(2,128)S(1)}, u32[]{:S(2)}) copy-start(f32[1,2,8,128]{3,1,2,0:T(2,128)S(1)} %copy.15) | copy-start | bytes 24580

commit v3 on v2

v3 whole, which is shorter than its diff:
```python
import functools

import jax
import jax.numpy as jnp
from jax import lax
from jax.experimental import pallas as pl
from jax.experimental.pallas import tpu as pltpu
from jax.sharding import Mesh, PartitionSpec as P

AXES = ("y", "xh", "xl", "z", "core")
IMAGES = 2048
FEAT = 2048
LOCAL = 16
GROUP = 512


BF = jnp.bfloat16
F32 = jnp.float32


def relu(values):
    return jnp.maximum(values, 0.0).astype(BF)


def dot(a, b):
    return jnp.dot(a, b, preferred_element_type=F32)


def pack(taps, head, joint, tail):
    tiles = []

    def split(values):
        tiles.extend(values[:, c : c + 128] for c in range(0, values.shape[1], 128))

    for t in range(0, taps - 1, 2):
        split(head(t))
        tiles.append(joint(t, t + 1))
        split(tail(t + 1))
    split(head(taps - 1))
    tiles.append(joint(taps - 1, taps - 1)[:, :64])
    return tiles


def contract(tiles, weights, fillers=(), step=4):
    values, row = None, 0
    groups = range(0, len(tiles), step)
    for n, first in enumerate(groups):
        part = jnp.concatenate(tiles[first : first + step], axis=1)
        product = dot(part, weights[row : row + part.shape[1]])
        row += part.shape[1]
        values = product if values is None else values + product
        for filler in fillers[len(fillers) * n // len(groups) : len(fillers) * (n + 1) // len(groups)]:
            filler()
    return values


def network_kernel(
    x_hbm,
    entry_hbm,
    wide_hbm,
    row_hbm,
    column_hbm,
    reduce_hbm,
    second_hbm,
    second_row_hbm,
    second_column_hbm,
    second_deep_hbm,
    deep_row_hbm,
    deep_column_hbm,
    pool_hbm,
    out,
    x,
    entry_w,
    wide_w,
    row_w,
    column_w,
    reduce_w,
    second_w,
    second_deep_w,
    branch_w,
    pool_w,
    long_head,
    long_joint,
    long_tail,
    row_head,
    row_joint,
    row_tail,
    short_head,
    short_ends,
    short_tail,
    tower_head,
    tower_ends,
    tower_tail,
    middle,
    branch,
    deep_head,
    deep_last,
    deep_first,
    deep_tail,
    averaged,
    branch_sums,
    features,
    sems,
):
    copies = {}

    def start(name, source, target, slot):
        copies[name] = pltpu.make_async_copy(source, target, sems.at[slot])
        copies[name].start()

    start("entry", entry_hbm, entry_w, 0)
    start("x0", x_hbm.at[pl.ds(0, 9)], x.at[pl.ds(0, 9)], 1)
    start("x1", x_hbm.at[pl.ds(9, 8)], x.at[pl.ds(9, 8)], 2)
    later = [
        ("row", row_hbm, row_w),
        ("column", column_hbm, column_w),
        ("wide", wide_hbm, wide_w),
        ("reduce", reduce_hbm, reduce_w),
        ("second", second_hbm, second_w),
        ("second_deep", second_deep_hbm, second_deep_w),
        ("second_row", second_row_hbm, branch_w.at[0]),
        ("second_column", second_column_hbm, branch_w.at[1]),
        ("deep_row", deep_row_hbm, branch_w.at[2]),
        ("deep_column", deep_column_hbm, branch_w.at[3]),
        ("pool", pool_hbm, pool_w),
    ]
    for i, (name, source, target) in enumerate(later):
        start(name, source, target, 3 + i)

    deep_last[...] = jnp.zeros((10, 10, LOCAL, 128), BF)
    deep_first[...] = jnp.zeros((10, 10, LOCAL, 128), BF)
    for array in (long_head, long_joint, long_tail):
        array[:, 0:3] = jnp.zeros((17, 3, LOCAL, 128), BF)
        array[:, 19:23] = jnp.zeros((17, 4, LOCAL, 128), BF)
    for array in (row_head, row_joint, row_tail):
        array[0:3] = jnp.zeros((3, 17, LOCAL, 128), BF)
        array[19:23] = jnp.zeros((4, 17, LOCAL, 128), BF)
    margins = [(middle, 1280), (deep_head, 384), (deep_tail, 384)]
    for array, channels in margins + [(branch.at[0], 384), (branch.at[1], 384)]:
        array[0] = jnp.zeros((10, LOCAL, channels), BF)
        array[9] = jnp.zeros((10, LOCAL, channels), BF)
        array[1:9, 0] = jnp.zeros((8, LOCAL, channels), BF)
        array[1:9, 9] = jnp.zeros((8, LOCAL, channels), BF)

    def split_by_parity(i, first, values, head, ends, tail):
        for r in range(first, first + 3):
            for c in range(17):
                at = (r % 2, c % 2, 4 * i + r // 2, c // 2)
                place = values[r - first, c]
                head[at] = place[:, 0:128]
                ends[(*at, slice(None), slice(0, 64))] = place[:, 128:192]
                ends[(*at, slice(None), slice(64, 128))] = place[:, 0:64]
                tail[at] = place[:, 64:192]

    def in_thirds(product, keep):
        earlier = product(0)
        for first in (3, 6):
            latter = product(first)
            keep(first - 3, earlier)
            earlier = latter
        keep(6, earlier)

    copies["entry"].wait()
    copies["x0"].wait()

    def entry_block(i, carry):
        @pl.when(i == 1)
        def _():
            copies["x1"].wait()

        def product(first):
            return dot(x[pl.ds(8 * i + first, 3)].reshape(816, 768), entry_w[...])

        def keep(first, values):
            values = relu(values).reshape(3, 17, LOCAL, 384)
            rows = pl.ds(8 * i + first, 3)
            long_head[rows, 3:20] = values[..., 192:320]
            long_joint[rows, 3:20, :, 0:64] = values[..., 320:384]
            long_joint[rows, 2:19, :, 64:128] = values[..., 192:256]
            long_tail[rows, 3:20] = values[..., 256:384]
            split_by_parity(i, first, values, short_head, short_ends, short_tail)

        in_thirds(product, keep)
        return carry

    lax.fori_loop(0, 2, entry_block, 0)

    copies["row"].wait()

    def maximum(i, r):
        tall = [
            jnp.maximum(
                jnp.maximum(x[8 * i + 2 * r, c], x[8 * i + 2 * r + 1, c]), x[8 * i + 2 * r + 2, c]
            )
            for c in range(17)
        ]
        for c in range(8):
            middle[4 * i + r + 1, c + 1, :, 512:] = jnp.maximum(
                jnp.maximum(tall[2 * c], tall[2 * c + 1]), tall[2 * c + 2]
            )

    def row_block(i, carry):
        def at(array, t):
            return array[pl.ds(8 * i, 9), t : t + 17].reshape(2448, 128)

        tiles = pack(
            7,
            lambda t: at(long_head, t),
            lambda t, u: at(long_joint, t),
            lambda t: at(long_tail, t),
        )
        fillers = [functools.partial(maximum, i, r) for r in range(4)]
        values = relu(contract(tiles, row_w, fillers)).reshape(9, 17, LOCAL, 192)
        row_head[pl.ds(8 * i + 3, 9)] = values[..., 0:128]
        row_joint[pl.ds(8 * i + 3, 9), :, :, 0:64] = values[..., 128:192]
        row_joint[pl.ds(8 * i + 2, 9), :, :, 64:128] = values[..., 0:64]
        row_tail[pl.ds(8 * i + 3, 9)] = values[..., 64:192]
        return carry

    lax.fori_loop(0, 2, row_block, 0)
    copies["column"].wait()

    def column_block(i, carry):
        def at(array, t):
            return array[pl.ds(8 * i + t, 9)].reshape(2448, 128)

        tiles = pack(
            7,
            lambda t: at(row_head, t),
            lambda t, u: at(row_joint, t),
            lambda t: at(row_tail, t),
        )
        values = relu(contract(tiles, column_w)).reshape(9, 17, LOCAL, 192)
        for first in (0, 3, 6):
            split_by_parity(
                i, first, values[first : first + 3], tower_head, tower_ends, tower_tail
            )
        return carry

    lax.fori_loop(0, 2, column_block, 0)
    copies["wide"].wait()
    copies["reduce"].wait()

    def half_map(step):
        lax.fori_loop(0, 2, lambda i, carry: step(4 * i), None)

    lower = lax.broadcasted_iota(jnp.int32, (512, 128), 1) < 64

    def joined(ends, t, u):
        return jnp.where(lower, ends(t), ends(u))

    def strided(arrays, weights, i):
        def at(array, t):
            a, b = t // 3, t % 3
            window = array[a % 2, b % 2, pl.ds(i + a // 2, 4), b // 2 : b // 2 + 8]
            return window.reshape(512, 128)

        head, ends, tail = (functools.partial(at, array) for array in arrays)
        return relu(contract(pack(9, head, functools.partial(joined, ends), tail), weights))

    def reduce_block(i):
        wide_out = strided((short_head, short_ends, short_tail), wide_w, i)
        middle[pl.ds(i + 1, 4), 1:9, :, 0:320] = wide_out.reshape(4, 8, LOCAL, 320)
        tower_out = strided((tower_head, tower_ends, tower_tail), reduce_w, i)
        middle[pl.ds(i + 1, 4), 1:9, :, 320:512] = tower_out.reshape(4, 8, LOCAL, 192)

    half_map(reduce_block)

    def add_sums(i, first, values):
        part = jnp.sum(values.astype(F32).reshape(32, LOCAL, -1), axis=0)
        at = slice(first, first + part.shape[1])
        features[:, at] = jnp.where(i == 0, 0.0, features[:, at]) + part

    copies["second"].wait()

    def second_block(i):
        flat = middle[pl.ds(i + 1, 4), 1:9].reshape(512, 1280)
        second = relu(dot(flat, second_w[...]))
        add_sums(i, 0, second[:, 0:320])
        rows = pl.ds(i + 1, 4)
        branch[0, rows, 1:9] = second[:, 320:704].reshape(4, 8, LOCAL, 384)
        deep_head[rows, 1:9] = second[:, 704:1088].reshape(4, 8, LOCAL, 384)
        deep_last[rows, 1:9, :, 0:64] = second[:, 1088:1152].reshape(4, 8, LOCAL, 64)
        deep_first[rows, 1:9, :, 64:128] = second[:, 704:768].reshape(4, 8, LOCAL, 64)
        deep_tail[rows, 1:9] = second[:, 768:1152].reshape(4, 8, LOCAL, 384)

    half_map(second_block)

    copies["second_deep"].wait()

    def average(i, r, first):
        at = slice(first, first + 256)
        edge = i + r == (0 if r < 2 else 7)
        columns = [
            middle[i + r, j, :, at].astype(F32)
            + middle[i + r + 1, j, :, at].astype(F32)
            + middle[i + r + 2, j, :, at].astype(F32)
            for j in range(10)
        ]
        for j in range(8):
            width = 3 - (j == 0) - (j == 7)
            scale = jnp.where(edge, 1.0 / (2 * width), 1.0 / (3 * width))
            box = (columns[j] + columns[j + 1] + columns[j + 2]) * scale
            averaged[i + r, j, :, at] = box.astype(BF)

    def deep_block(i):
        def at(array, t):
            window = array[pl.ds(i + t // 3, 4), t % 3 : t % 3 + 8]
            return window.reshape(512, array.shape[3])

        tiles = pack(
            9,
            lambda t: at(deep_head, t),
            lambda t, u: at(deep_last, t) + at(deep_first, u),
            lambda t: at(deep_tail, t),
        )
        fillers = [functools.partial(average, i, r, 256 * n) for n in range(5) for r in range(4)]
        values = relu(contract(tiles, second_deep_w, fillers))
        branch[1, pl.ds(i + 1, 4), 1:9] = values.reshape(4, 8, LOCAL, 384)

    half_map(deep_block)
    for name in ("second_row", "second_column", "deep_row", "deep_column"):
        copies[name].wait()

    def branch_map(n, carry):
        def tap(t):
            down, right = jnp.where(n % 2 == 0, 1, t), jnp.where(n % 2 == 0, t, 1)
            return branch[n // 2, pl.ds(down, 8), pl.ds(right, 8)].reshape(1024, 384)

        values = relu(dot(jnp.concatenate([tap(t) for t in range(3)], axis=1), branch_w[n]))
        branch_sums[n] = jnp.sum(values.astype(F32).reshape(64, LOCAL, 384), axis=0)
        return carry

    lax.fori_loop(0, 4, branch_map, 0)
    for n in range(4):
        features[:, 320 + 384 * n : 704 + 384 * n] = branch_sums[n]
    copies["pool"].wait()

    def pool_block(i):
        pooled = lax.dot_general(
            averaged[pl.ds(i, 4)].reshape(512, 1280),
            pool_w[...],
            (((1,), (1,)), ((), ())),
            preferred_element_type=F32,
        )
        add_sums(i, 1856, relu(pooled))

    half_map(pool_block)

    for block in range(16):
        part = features[:, 128 * block : 128 * block + 128] * (1.0 / 64.0)
        total = jnp.sum(part, axis=0, keepdims=True)
        for target in range(16):
            target_x, target_z = target // 4, target % 4
            if block % 4 == target_x:
                out[target, :, 128 * (block // 4) : 128 * (block // 4) + 128] = part
            if block // 4 == target_z:
                out[target, :, 512 + 128 * (block % 4) : 640 + 128 * (block % 4)] = part
            out[target, block : block + 1, 1024:1152] = total


def network(
    block_inputs,
    first_entry,
    first_wide,
    first_row,
    first_column,
    first_reduce,
    second_entry,
    second_row,
    second_column,
    second_deep,
    deep_row,
    deep_column,
    pool_project,
):
    operands = (
        block_inputs.transpose(1, 2, 0, 3),
        first_entry[0, 0],
        first_wide.reshape(1728, 320),
        first_row.reshape(1344, 192),
        first_column.reshape(1344, 192),
        first_reduce.reshape(1728, 192),
        second_entry[0, 0],
        second_row.reshape(1152, 384),
        second_column.reshape(1152, 384),
        second_deep.reshape(4032, 384),
        deep_row.reshape(1152, 384),
        deep_column.reshape(1152, 384),
        pool_project[0, 0].T,
    )
    place = lambda *shape: pltpu.VMEM(shape, BF)
    return pl.pallas_call(
        network_kernel,
        out_shape=jax.ShapeDtypeStruct((16, LOCAL, 1152), F32),
        in_specs=[pl.BlockSpec(memory_space=pl.ANY)] * 13,
        out_specs=pl.BlockSpec(memory_space=pltpu.VMEM),
        scratch_shapes=[place(*a.shape) for a in operands[:7]]
        + [place(4032, 384), place(4, 1152, 384), place(192, 1280)]
        + [place(17, 23, LOCAL, 128)] * 3
        + [place(23, 17, LOCAL, 128)] * 3
        + [place(2, 2, 9, 9, LOCAL, 128)] * 6
        + [
            place(10, 10, LOCAL, 1280),
            place(2, 10, 10, LOCAL, 384),
            place(10, 10, LOCAL, 384),
            place(10, 10, LOCAL, 128),
            place(10, 10, LOCAL, 128),
            place(10, 10, LOCAL, 384),
            place(8, 8, LOCAL, 1280),
            pltpu.VMEM((4, LOCAL, 384), F32),
            pltpu.VMEM((LOCAL, 2048), F32),
            pltpu.SemaphoreType.DMA((14,)),
        ],
        compiler_params=pltpu.CompilerParams(vmem_limit_bytes=67043328),
        cost_estimate=pl.CostEstimate(
            flops=19600000000, bytes_accessed=21000000, transcendentals=0
        ),
        name="network",
    )(*operands)


def cut(array, index, size, axis):
    return lax.dynamic_slice_in_dim(array, index * size, size, axis)


def statistics(message):
    highest = lax.Precision.HIGHEST
    x = lax.axis_index("xh") * 2 + lax.axis_index("xl")
    core = lax.axis_index("core")
    row_block = lax.axis_index("y") * 4 + x
    col_block = lax.axis_index("z") * 2 + core
    got = lax.all_to_all(message, ("xh", "xl", "z"), 0, 0, tiled=True)
    half_sum = jnp.sum(got[:, :, 1024:], axis=0)
    other_columns = lax.dynamic_slice_in_dim(got, 512 + 256 * (1 - core), 256, 2)
    pass_on = jnp.concatenate([got[:, :, :512], other_columns], -1).reshape(256, 768)
    pass_on = jnp.concatenate(
        [pass_on, jnp.pad(half_sum, ((0, 0), (0, 640)))], 0
    )
    passed = lax.ppermute(pass_on, "core", [(0, 1), (1, 0)])
    group_mean = (half_sum + passed[256:, :128]).reshape(FEAT) / GROUP
    own_columns = lax.dynamic_slice_in_dim(got, 512 + 256 * core, 256, 2).reshape(256, 256)
    rows_mean = lax.dynamic_index_in_dim(group_mean.reshape(4, 4, 128), x, 1, False).reshape(512)
    centered_rows = (
        jnp.concatenate([got[:, :, :512].reshape(256, 512), passed[:256, :512]], 0) - rows_mean
    )
    centered_columns = jnp.concatenate([own_columns, passed[:256, 512:]], 0) - cut(
        group_mean, col_block, 256, 0
    )
    moments = jnp.einsum(
        "nf,nc->fc",
        centered_rows,
        centered_columns,
        precision=highest,
        preferred_element_type=jnp.float32,
    )
    parts = jnp.concatenate(
        [
            moments.reshape(4, 128, 256),
            jnp.broadcast_to(group_mean.reshape(1, 8, 256), (4, 8, 256)),
        ],
        axis=1,
    )
    parts = lax.all_to_all(parts, "y", 0, 0, tiled=True)
    means = parts[:, 128:].reshape(4, FEAT)
    feature_mean = jnp.sum(means, axis=0) / 4
    gap = means - feature_mean
    between = jnp.einsum(
        "gf,gc->fc",
        cut(gap, row_block, 128, 1),
        cut(gap, col_block, 256, 1),
        precision=highest,
        preferred_element_type=jnp.float32,
    )
    covariance = (jnp.sum(parts[:, :128], axis=0) + between * GROUP) / (IMAGES - 1)
    return feature_mean, covariance


def local(*arguments):
    return statistics(network(*arguments))


def solution(mesh):
    fine = Mesh(mesh.devices.reshape(4, 2, 2, 4, 2), AXES)
    placed = (P(AXES, None, None, None),) + (P(),) * 12
    return jax.shard_map(
        local,
        mesh=fine,
        in_specs=placed,
        out_specs=(P(), P(("y", "xh", "xl"), ("z", "core"))),
        check_vma=False,
    )
```

time: 100 us -> 87.5 us (0.88)
  Pallas kernels: 50.7 us -> 38 us
    pallas_call x1, Pallas kernels: 50.7 us -> 38 us  [network(): pl.pallas_call(network_kernel, out_shape=jax.ShapeDtypeStruct((16, LOCAL,...]
where the time goes in v3:
time: 87.5 us; the launch traced here: 87.2 us
  Pallas kernels  38 us (43%)
  waiting for transfers between devices  28.2 us (32%)
  starting transfers between devices  16 us (18%)
  matrix products  2.82 us (3%)
  other arithmetic  1.04 us (1%)
    pallas_call x1, Pallas kernels, network(): pl.pallas_call(network_kernel, out_shape=jax.ShapeDtypeStruct((16, LOCAL,...  38 us
    all_to_all x1, waiting for transfers between devices, statistics(): got = lax.all_to_all(message, ('xh', 'xl', 'z'), 0, 0, tiled=True)  17 us
    all_to_all x1, waiting for transfers between devices, statistics(): parts = lax.all_to_all(parts, 'y', 0, 0, tiled=True)  9.26 us
    all_to_all x1, starting transfers between devices, statistics(): got = lax.all_to_all(message, ('xh', 'xl', 'z'), 0, 0, tiled=True)  8.43 us
    all_to_all x1, starting transfers between devices, statistics(): parts = lax.all_to_all(parts, 'y', 0, 0, tiled=True)  4.19 us
    ppermute x1, starting transfers between devices, statistics(): passed = lax.ppermute(pass_on, 'core', [(0, 1), (1, 0)])  3.34 us
    ppermute x1, waiting for transfers between devices, statistics(): passed = lax.ppermute(pass_on, 'core', [(0, 1), (1, 0)])  1.98 us
    dot_general x1, matrix products, statistics(): jnp.einsum('nf,nc->fc', centered_rows, centered_columns, precision=highes...  1.82 us
  transfers between devices with their start and end apart: 3, of which 3 were waited for; matrix products, arithmetic and copies ran while one was open for 0% of the time, Pallas kernels for 0%

profile of v3, /device:TPU:1, one launch (start us, length us, event | category | flops | bytes accessed | tf_op | source)
XLA Modules:
  0.0 87.2 jit_solution(17620213391992811794)
XLA Ops:
  0.6 38.0 %network.1 = f32[16,16,1152]{2,1,0:T(8,128)} custom-call(bf16[17,17,16,768]{3,2,1,0:T(8,128)(2,1)} %bitcast.38, bf16[768,384]{1,0:T(8,128)(2,1)} %bitcast.49, bf16[1728,320]{1,0:T(8,128)(2,1)} %bitcast.41, bf16[1344,192]{1,0:T(8,128)(2,1)} %bitcast.47, bf16[1344,192]{1,0:T(8,128)(2,1)} %bitcast.48, bf16[1728,192]{1,0:T(8,128)(2,1)} %bitcast.42, ...), custom_call_target="tpu_custom_call" | custom-call | flops 19599998976 | bytes 21000000 | tf_op jit(solution)/shard_map/network/pallas_call | solution.py:393
  38.7 8.4 %all-to-all-start = ((f32[16,16,1152]{2,1,0:T(8,128)}), f32[16,16,1152]{2,1,0:T(8,128)S(1)}, u32[]{:S(2)}, u32[]{:S(2)}) async-start(f32[16,16,1152]{2,1,0:T(8,128)} %network.1), calls=%async_computation | async-start | bytes 2359296 | tf_op jit(solution)/shard_map/all_to_all | solution.py:433
  47.1 17.0 %all-to-all-done = f32[16,16,1152]{2,1,0:T(8,128)S(1)} async-done(((f32[16,16,1152]{2,1,0:T(8,128)}), f32[16,16,1152]{2,1,0:T(8,128)S(1)}, u32[]{:S(2)}, u32[]{:S(2)}) %all-to-all-start) | async-done | bytes 1179680 | tf_op jit(solution)/shard_map/all_to_all | solution.py:433
  64.2 0.1 constant_dynamic-slice_fusion
  64.2 0.1 pad_maximum_fusion
  64.3 0.1 select_maximum_fusion
  64.4 3.3 %collective-permute-start = (f32[272,768]{1,0:T(8,128)S(1)}, f32[272,768]{1,0:T(8,128)S(1)}, u32[]{:S(2)}, u32[]{:S(2)}) collective-permute-start(f32[272,768]{1,0:T(8,128)S(1)} %select_maximum_fusion), channel_id=1, source_target_pairs={{0,1},{1,0},{2,3},{3,2},{4,5},{5,4},{6,7},{7,6},{8,9},{9,8},{10,11... | collective-permute-start | bytes 2506760 | tf_op jit(solution)/shard_map/ppermute | solution.py:440
  67.7 2.0 %collective-permute-done = f32[272,768]{1,0:T(8,128)S(1)} collective-permute-done((f32[272,768]{1,0:T(8,128)S(1)}, f32[272,768]{1,0:T(8,128)S(1)}, u32[]{:S(2)}, u32[]{:S(2)}) %collective-permute-start) | collective-permute-done | bytes 835616 | tf_op jit(solution)/shard_map/ppermute | solution.py:440
  69.7 0.1 dynamic_slice.22
  69.8 0.1 slice.31
  69.9 1.8 %fusion.2 = f32[512,256]{1,0:T(8,128)S(1)} fusion(f32[256,512]{1,0:T(8,128)S(1)} %slice.31, f32[256,512]{1,0:T(8,128)S(1)} %bitcast.28, f32[256,256]{1,0:T(8,128)S(1)} %slice.33, f32[256,256]{1,0:T(8,128)S(1)} %bitcast.31, f32[512]{0:T(512)S(1)} %bitcast.37, f32[256]{0:T(256)S(1)} %dynamic_slice.22), kind=kOutput, calls=%fused_computation.4 | convolution fusion | flops 806092800 | bytes 2100224 | tf_op jit(solution)/shard_map/nf,nc->fc/dot_general | solution.py:450
  71.8 0.8 pad_maximum_fusion.1
  72.6 4.2 %all-to-all-start.1 = ((f32[4,136,256]{2,1,0:T(8,128)}), f32[4,136,256]{2,1,0:T(8,128)S(1)}, u32[]{:S(2)}, u32[]{:S(2)}) async-start(f32[4,136,256]{2,1,0:T(8,128)} %pad_maximum_fusion.1), calls=%async_computation.1 | async-start | bytes 1114112 | tf_op jit(solution)/shard_map/all_to_all | solution.py:464
  76.8 9.3 %all-to-all-done.1 = f32[4,136,256]{2,1,0:T(8,128)S(1)} async-done(((f32[4,136,256]{2,1,0:T(8,128)}), f32[4,136,256]{2,1,0:T(8,128)S(1)}, u32[]{:S(2)}, u32[]{:S(2)}) %all-to-all-start.1) | async-done | bytes 557088 | tf_op jit(solution)/shard_map/all_to_all | solution.py:464
  86.1 0.0 copy-start
  86.2 1.0 %fusion.1 = f32[128,256]{1,0:T(8,128)} fusion(f32[128,256]{1,0:T(8,128)S(1)} %slice_reduce_fusion, f32[4,2048]{1,0:T(4,128)S(1)} %broadcast_subtract_fusion, s32[]{:T(128)S(6)} %select_n.20, s32[]{:T(128)S(6)} %select_n.21), kind=kOutput, calls=%fused_computation.2 | convolution fusion | flops 1671168 | bytes 268296 | tf_op jit(solution)/shard_map/gf,gc->fc/dot_general | solution.py:468
  87.2 0.0 copy-done
  (13 shorter events, 0.2 us)
Async XLA Ops:
  38.7 25.4 %all-to-all-start = ((f32[16,16,1152]{2,1,0:T(8,128)}), f32[16,16,1152]{2,1,0:T(8,128)S(1)}, u32[]{:S(2)}, u32[]{:S(2)}) async-start(f32[16,16,1152]{2,1,0:T(8,128)} %network.1), calls=%async_computation | async-start | bytes 2359296 | tf_op jit(solution)/shard_map/all_to_all | solution.py:433
  64.4 5.3 %collective-permute-start = (f32[272,768]{1,0:T(8,128)S(1)}, f32[272,768]{1,0:T(8,128)S(1)}, u32[]{:S(2)}, u32[]{:S(2)}) collective-permute-start(f32[272,768]{1,0:T(8,128)S(1)} %select_maximum_fusion), channel_id=1, source_target_pairs={{0,1},{1,0},{2,3},{3,2},{4,5},{5,4},{6,7},{7,6},{8,9},{9,8},{10,11... | collective-permute-start | bytes 2506760 | tf_op jit(solution)/shard_map/ppermute | solution.py:440
  72.6 13.4 %all-to-all-start.1 = ((f32[4,136,256]{2,1,0:T(8,128)}), f32[4,136,256]{2,1,0:T(8,128)S(1)}, u32[]{:S(2)}, u32[]{:S(2)}) async-start(f32[4,136,256]{2,1,0:T(8,128)} %pad_maximum_fusion.1), calls=%async_computation.1 | async-start | bytes 1114112 | tf_op jit(solution)/shard_map/all_to_all | solution.py:464
  86.1 1.1 %copy-start = (f32[1,2,8,128]{3,1,2,0:T(2,128)}, f32[1,2,8,128]{3,1,2,0:T(2,128)S(1)}, u32[]{:S(2)}) copy-start(f32[1,2,8,128]{3,1,2,0:T(2,128)S(1)} %copy.15) | copy-start | bytes 24580

commit v4 on v3

--- a/solution.py
+++ b/solution.py
@@ -102,15 +102,25 @@
     features,
     sems,
 ):
-    copies = {}
-
-    def start(name, source, target, slot):
-        copies[name] = pltpu.make_async_copy(source, target, sems.at[slot])
-        copies[name].start()
-
-    start("entry", entry_hbm, entry_w, 0)
-    start("x0", x_hbm.at[pl.ds(0, 9)], x.at[pl.ds(0, 9)], 1)
-    start("x1", x_hbm.at[pl.ds(9, 8)], x.at[pl.ds(9, 8)], 2)
+    def copy(name):
+        source, target, slot = moves[name]
+        return pltpu.make_async_copy(source, target, sems.at[slot])
+
+    moves = {"entry": (entry_hbm, entry_w, 0)}
+    copy("entry").start()
+    def x_third(i, first):
+        source = x_hbm.at[pl.ds(8 * i + first, 3)]
+        target = x.at[pl.ds(9 * i + first, 3)]
+        return pltpu.make_async_copy(source, target, sems.at[1 + 3 * i + first // 3])
+
+    for i in range(2):
+        for first in (0, 3, 6):
+            x_third(i, first).start()
+
+    def start_later():
+        for name, _, _ in later:
+            copy(name).start()
+
     later = [
         ("row", row_hbm, row_w),
         ("column", column_hbm, column_w),
@@ -125,7 +135,7 @@
         ("pool", pool_hbm, pool_w),
     ]
     for i, (name, source, target) in enumerate(later):
-        start(name, source, target, 3 + i)
+        moves[name] = (source, target, 7 + i)
 
     deep_last[...] = jnp.zeros((10, 10, LOCAL, 128), BF)
     deep_first[...] = jnp.zeros((10, 10, LOCAL, 128), BF)
@@ -160,16 +170,16 @@
             earlier = latter
         keep(6, earlier)
 
-    copies["entry"].wait()
-    copies["x0"].wait()
+    copy("entry").wait()
 
     def entry_block(i, carry):
         @pl.when(i == 1)
         def _():
-            copies["x1"].wait()
+            start_later()
 
         def product(first):
-            return dot(x[pl.ds(8 * i + first, 3)].reshape(816, 768), entry_w[...])
+            x_third(i, first).wait()
+            return dot(x[pl.ds(9 * i + first, 3)].reshape(816, 768), entry_w[...])
 
         def keep(first, values):
             values = relu(values).reshape(3, 17, LOCAL, 384)
@@ -185,12 +195,12 @@
 
     lax.fori_loop(0, 2, entry_block, 0)
 
-    copies["row"].wait()
+    copy("row").wait()
 
     def maximum(i, r):
         tall = [
             jnp.maximum(
-                jnp.maximum(x[8 * i + 2 * r, c], x[8 * i + 2 * r + 1, c]), x[8 * i + 2 * r + 2, c]
+                jnp.maximum(x[9 * i + 2 * r, c], x[9 * i + 2 * r + 1, c]), x[9 * i + 2 * r + 2, c]
             )
             for c in range(17)
         ]
@@ -218,7 +228,7 @@
         return carry
 
     lax.fori_loop(0, 2, row_block, 0)
-    copies["column"].wait()
+    copy("column").wait()
 
     def column_block(i, carry):
         def at(array, t):
@@ -238,8 +248,8 @@
         return carry
 
     lax.fori_loop(0, 2, column_block, 0)
-    copies["wide"].wait()
-    copies["reduce"].wait()
+    copy("wide").wait()
+    copy("reduce").wait()
 
     def half_map(step):
         lax.fori_loop(0, 2, lambda i, carry: step(4 * i), None)
@@ -271,7 +281,7 @@
         at = slice(first, first + part.shape[1])
         features[:, at] = jnp.where(i == 0, 0.0, features[:, at]) + part
 
-    copies["second"].wait()
+    copy("second").wait()
 
     def second_block(i):
         flat = middle[pl.ds(i + 1, 4), 1:9].reshape(512, 1280)
@@ -286,7 +296,8 @@
 
     half_map(second_block)
 
-    copies["second_deep"].wait()
+    copy("second_deep").wait()
+    copy("pool").wait()
 
     def average(i, r, first):
         at = slice(first, first + 256)
@@ -315,28 +326,8 @@
             lambda t: at(deep_tail, t),
         )
         fillers = [functools.partial(average, i, r, 256 * n) for n in range(5) for r in range(4)]
-        values = relu(contract(tiles, second_deep_w, fillers))
+        values = relu(contract(tiles, second_deep_w, fillers, 8))
         branch[1, pl.ds(i + 1, 4), 1:9] = values.reshape(4, 8, LOCAL, 384)
-
-    half_map(deep_block)
-    for name in ("second_row", "second_column", "deep_row", "deep_column"):
-        copies[name].wait()
-
-    def branch_map(n, carry):
-        def tap(t):
-            down, right = jnp.where(n % 2 == 0, 1, t), jnp.where(n % 2 == 0, t, 1)
-            return branch[n // 2, pl.ds(down, 8), pl.ds(right, 8)].reshape(1024, 384)
-
-        values = relu(dot(jnp.concatenate([tap(t) for t in range(3)], axis=1), branch_w[n]))
-        branch_sums[n] = jnp.sum(values.astype(F32).reshape(64, LOCAL, 384), axis=0)
-        return carry
-
-    lax.fori_loop(0, 4, branch_map, 0)
-    for n in range(4):
-        features[:, 320 + 384 * n : 704 + 384 * n] = branch_sums[n]
-    copies["pool"].wait()
-
-    def pool_block(i):
         pooled = lax.dot_general(
             averaged[pl.ds(i, 4)].reshape(512, 1280),
             pool_w[...],
@@ -345,18 +336,36 @@
         )
         add_sums(i, 1856, relu(pooled))
 
-    half_map(pool_block)
-
+    half_map(deep_block)
+    for name in ("second_row", "second_column", "deep_row", "deep_column"):
+        copy(name).wait()
+
+    def branch_map(n, carry):
+        def tap(t):
+            down, right = jnp.where(n % 2 == 0, 1, t), jnp.where(n % 2 == 0, t, 1)
+            return branch[n // 2, pl.ds(down, 8), pl.ds(right, 8)].reshape(1024, 384)
+
+        values = relu(dot(jnp.concatenate([tap(t) for t in range(3)], axis=1), branch_w[n]))
+        branch_sums[n] = jnp.sum(values.astype(F32).reshape(64, LOCAL, 384), axis=0)
+        return carry
+
+    lax.fori_loop(0, 4, branch_map, 0)
+    for n in range(4):
+        features[:, 320 + 384 * n : 704 + 384 * n] = branch_sums[n]
     for block in range(16):
         part = features[:, 128 * block : 128 * block + 128] * (1.0 / 64.0)
         total = jnp.sum(part, axis=0, keepdims=True)
+        own_y, own_x = block // 4, block % 4
         for target in range(16):
             target_x, target_z = target // 4, target % 4
-            if block % 4 == target_x:
-                out[target, :, 128 * (block // 4) : 128 * (block // 4) + 128] = part
-            if block // 4 == target_z:
-                out[target, :, 512 + 128 * (block % 4) : 640 + 128 * (block % 4)] = part
-            out[target, block : block + 1, 1024:1152] = total
+            slot = None
+            if own_y == target_z:
+                slot = own_x
+            elif own_x == target_x:
+                slot = 4 + own_y - (own_y > target_z)
+            if slot is not None:
+                out[target, :, 128 * slot : 128 * slot + 128] = part
+            out[target, block : block + 1, 896:1024] = total
 
 
 def network(
@@ -392,10 +401,11 @@
     place = lambda *shape: pltpu.VMEM(shape, BF)
     return pl.pallas_call(
         network_kernel,
-        out_shape=jax.ShapeDtypeStruct((16, LOCAL, 1152), F32),
+        out_shape=jax.ShapeDtypeStruct((16, LOCAL, 1024), F32),
         in_specs=[pl.BlockSpec(memory_space=pl.ANY)] * 13,
         out_specs=pl.BlockSpec(memory_space=pltpu.VMEM),
-        scratch_shapes=[place(*a.shape) for a in operands[:7]]
+        scratch_shapes=[place(18, 17, LOCAL, 768)]
+        + [place(*a.shape) for a in operands[1:7]]
         + [place(4032, 384), place(4, 1152, 384), place(192, 1280)]
         + [place(17, 23, LOCAL, 128)] * 3
         + [place(23, 17, LOCAL, 128)] * 3
@@ -410,7 +420,7 @@
             place(8, 8, LOCAL, 1280),
             pltpu.VMEM((4, LOCAL, 384), F32),
             pltpu.VMEM((LOCAL, 2048), F32),
-            pltpu.SemaphoreType.DMA((14,)),
+            pltpu.SemaphoreType.DMA((18,)),
         ],
         compiler_params=pltpu.CompilerParams(vmem_limit_bytes=67043328),
         cost_estimate=pl.CostEstimate(
@@ -427,23 +437,32 @@
 def statistics(message):
     highest = lax.Precision.HIGHEST
     x = lax.axis_index("xh") * 2 + lax.axis_index("xl")
+    y = lax.axis_index("y")
+    z = lax.axis_index("z")
     core = lax.axis_index("core")
-    row_block = lax.axis_index("y") * 4 + x
-    col_block = lax.axis_index("z") * 2 + core
+    row_block = y * 4 + x
+    col_block = z * 2 + core
     got = lax.all_to_all(message, ("xh", "xl", "z"), 0, 0, tiled=True)
-    half_sum = jnp.sum(got[:, :, 1024:], axis=0)
-    other_columns = lax.dynamic_slice_in_dim(got, 512 + 256 * (1 - core), 256, 2)
-    pass_on = jnp.concatenate([got[:, :, :512], other_columns], -1).reshape(256, 768)
-    pass_on = jnp.concatenate(
-        [pass_on, jnp.pad(half_sum, ((0, 0), (0, 640)))], 0
-    )
+    half_sum = jnp.sum(got[:, :, 896:], axis=0)
+    shared = lax.dynamic_slice_in_dim(got, 128 * x, 128, 2)
+    others = [got[:, :, 512 + 128 * n : 640 + 128 * n] for n in range(3)]
+    rows = jnp.concatenate(
+        [
+            jnp.where(
+                z == n, shared, jnp.where(n < z, others[min(n, 2)], others[max(n - 1, 0)])
+            )
+            for n in range(4)
+        ],
+        axis=-1,
+    )
+    other_columns = lax.dynamic_slice_in_dim(got, 256 * (1 - core), 256, 2)
+    pass_on = jnp.concatenate([rows, other_columns], -1).reshape(256, 768)
+    pass_on = jnp.concatenate([pass_on, jnp.pad(half_sum, ((0, 0), (0, 640)))], 0)
     passed = lax.ppermute(pass_on, "core", [(0, 1), (1, 0)])
     group_mean = (half_sum + passed[256:, :128]).reshape(FEAT) / GROUP
-    own_columns = lax.dynamic_slice_in_dim(got, 512 + 256 * core, 256, 2).reshape(256, 256)
+    own_columns = lax.dynamic_slice_in_dim(got, 256 * core, 256, 2).reshape(256, 256)
     rows_mean = lax.dynamic_index_in_dim(group_mean.reshape(4, 4, 128), x, 1, False).reshape(512)
-    centered_rows = (
-        jnp.concatenate([got[:, :, :512].reshape(256, 512), passed[:256, :512]], 0) - rows_mean
-    )
+    centered_rows = jnp.concatenate([rows.reshape(256, 512), passed[:256, :512]], 0) - rows_mean
     centered_columns = jnp.concatenate([own_columns, passed[:256, 512:]], 0) - cut(
         group_mean, col_block, 256, 0
     )
@@ -461,10 +480,14 @@
         ],
         axis=1,
     )
-    parts = lax.all_to_all(parts, "y", 0, 0, tiled=True)
-    means = parts[:, 128:].reshape(4, FEAT)
-    feature_mean = jnp.sum(means, axis=0) / 4
-    gap = means - feature_mean
+    exchanged = [lax.dynamic_index_in_dim(parts, y, 0, False)]
+    for n in (1, 3, 2):
+        part = lax.dynamic_index_in_dim(parts, y ^ n, 0, False)
+        exchanged.append(lax.ppermute(part, "y", [(k, k ^ n) for k in range(4)]))
+    own, near, wrap, far = exchanged
+    total = (own + near) + (far + wrap)
+    feature_mean = total[128:].reshape(FEAT) / 4
+    gap = jnp.stack([part[128:].reshape(FEAT) for part in exchanged]) - feature_mean
     between = jnp.einsum(
         "gf,gc->fc",
         cut(gap, row_block, 128, 1),
@@ -472,7 +495,7 @@
         precision=highest,
         preferred_element_type=jnp.float32,
     )
-    covariance = (jnp.sum(parts[:, :128], axis=0) + between * GROUP) / (IMAGES - 1)
+    covariance = (total[:128] + between * GROUP) / (IMAGES - 1)
     return feature_mean, covariance
 
 

time: 87.5 us -> 83.8 us (0.958)
  waiting for transfers between devices: 28.2 us -> 26.5 us
    all_to_all x1 -> x0, waiting for transfers between devices: 9.26 us -> none  [statistics(): parts = lax.all_to_all(parts, 'y', 0, 0, tiled=True)]
    ppermute x0 -> x3, waiting for transfers between devices: none -> 8.94 us  [statistics(): exchanged.append(lax.ppermute(part, 'y', [(k, k ^ n) for k in range(4)]))]
    all_to_all x1 -> x0, starting transfers between devices: 4.19 us -> none  [statistics(): parts = lax.all_to_all(parts, 'y', 0, 0, tiled=True)]
    ppermute x0 -> x3, starting transfers between devices: none -> 4.01 us  [statistics(): exchanged.append(lax.ppermute(part, 'y', [(k, k ^ n) for k in range(4)]))]
    all_to_all x1, waiting for transfers between devices: 17 us -> 15.6 us  [statistics(): got = lax.all_to_all(message, ('xh', 'xl', 'z'), 0, 0, tiled=True)]
  transfers between devices with their start and end apart: 3 -> 5, of which waited for: 3 -> 5; matrix products, arithmetic and copies ran while one was open for 0% -> 0% of each run, Pallas kernels for 0% -> 0%
where the time goes in v4:
time: 83.8 us; the launch traced here: 83.6 us
  Pallas kernels  37.2 us (44%)
  waiting for transfers between devices  26.5 us (32%)
  starting transfers between devices  15.6 us (19%)
  matrix products  2.82 us (3%)
  between operations  0.86 us (1%)
    pallas_call x1, Pallas kernels, network(): pl.pallas_call(network_kernel, out_shape=jax.ShapeDtypeStruct((16, LOCAL,...  37.2 us
    all_to_all x1, waiting for transfers between devices, statistics(): got = lax.all_to_all(message, ('xh', 'xl', 'z'), 0, 0, tiled=True)  15.6 us
    ppermute x3, waiting for transfers between devices, statistics(): exchanged.append(lax.ppermute(part, 'y', [(k, k ^ n) for k in range(4)]))  8.94 us
    all_to_all x1, starting transfers between devices, statistics(): got = lax.all_to_all(message, ('xh', 'xl', 'z'), 0, 0, tiled=True)  8.43 us
    ppermute x3, starting transfers between devices, statistics(): exchanged.append(lax.ppermute(part, 'y', [(k, k ^ n) for k in range(4)]))  4.01 us
    ppermute x1, starting transfers between devices, statistics(): passed = lax.ppermute(pass_on, 'core', [(0, 1), (1, 0)])  3.12 us
    ppermute x1, waiting for transfers between devices, statistics(): passed = lax.ppermute(pass_on, 'core', [(0, 1), (1, 0)])  1.94 us
    dot_general x1, matrix products, statistics(): jnp.einsum('nf,nc->fc', centered_rows, centered_columns, precision=highes...  1.82 us
  transfers between devices with their start and end apart: 5, of which 5 were waited for; matrix products, arithmetic and copies ran while one was open for 0% of the time, Pallas kernels for 0%

profile of v4, /device:TPU:1, one launch (start us, length us, event | category | flops | bytes accessed | tf_op | source)
XLA Modules:
  0.0 83.6 jit_solution(2947281881374972561)
XLA Ops:
  0.6 37.2 %network.1 = f32[16,16,1024]{2,1,0:T(8,128)} custom-call(bf16[17,17,16,768]{3,2,1,0:T(8,128)(2,1)} %bitcast.64, bf16[768,384]{1,0:T(8,128)(2,1)} %bitcast.75, bf16[1728,320]{1,0:T(8,128)(2,1)} %bitcast.67, bf16[1344,192]{1,0:T(8,128)(2,1)} %bitcast.73, bf16[1344,192]{1,0:T(8,128)(2,1)} %bitcast.74, bf16[1728,192]{1,0:T(8,128)(2,1)} %bitcast.68, ...), custom_call_target="tpu_custom_call" | custom-call | flops 19599998976 | bytes 21000000 | tf_op jit(solution)/shard_map/network/pallas_call | solution.py:402
  37.8 8.4 %all-to-all-start = ((f32[16,16,1024]{2,1,0:T(8,128)}), f32[16,16,1024]{2,1,0:T(8,128)S(1)}, u32[]{:S(2)}, u32[]{:S(2)}) async-start(f32[16,16,1024]{2,1,0:T(8,128)} %network.1), calls=%async_computation | async-start | bytes 2097152 | tf_op jit(solution)/shard_map/all_to_all | solution.py:445
  46.3 15.6 %all-to-all-done = f32[16,16,1024]{2,1,0:T(8,128)S(1)} async-done(((f32[16,16,1024]{2,1,0:T(8,128)}), f32[16,16,1024]{2,1,0:T(8,128)S(1)}, u32[]{:S(2)}, u32[]{:S(2)}) %all-to-all-start) | async-done | bytes 1048608 | tf_op jit(solution)/shard_map/all_to_all | solution.py:445
  62.1 0.1 select_maximum_fusion
  62.2 3.1 %collective-permute-start = (f32[272,768]{1,0:T(8,128)S(1)}, f32[272,768]{1,0:T(8,128)S(1)}, u32[]{:S(2)}, u32[]{:S(2)}) collective-permute-start(f32[272,768]{1,0:T(8,128)S(1)} %select_maximum_fusion), channel_id=1, source_target_pairs={{0,1},{1,0},{2,3},{3,2},{4,5},{5,4},{6,7},{7,6},{8,9},{9,8},{10,11... | collective-permute-start | bytes 2506760 | tf_op jit(solution)/shard_map/ppermute | solution.py:461
  65.4 1.9 %collective-permute-done = f32[272,768]{1,0:T(8,128)S(1)} collective-permute-done((f32[272,768]{1,0:T(8,128)S(1)}, f32[272,768]{1,0:T(8,128)S(1)}, u32[]{:S(2)}, u32[]{:S(2)}) %collective-permute-start) | collective-permute-done | bytes 835616 | tf_op jit(solution)/shard_map/ppermute | solution.py:461
  67.3 0.1 dynamic_slice.39
  67.4 0.1 slice.57
  67.5 1.8 %fusion = f32[512,256]{1,0:T(8,128)S(1)} fusion(f32[256,512]{1,0:T(8,128)S(1)} %slice.57, f32[256,512]{1,0:T(8,128)S(1)} %bitcast.52, f32[256,256]{1,0:T(8,128)S(1)} %slice.59, f32[256,256]{1,0:T(8,128)S(1)} %bitcast.54, f32[512]{0:T(512)S(1)} %bitcast.63, f32[256]{0:T(256)S(1)} %dynamic_slice.39), kind=kOutput, calls=%fused_computation.6 | convolution fusion | flops 806092800 | bytes 2100224 | tf_op jit(solution)/shard_map/nf,nc->fc/dot_general | solution.py:469
  69.4 1.4 %collective-permute-start.1 = (f32[136,256]{1,0:T(8,128)S(1)}, f32[136,256]{1,0:T(8,128)S(1)}, u32[]{:S(2)}, u32[]{:S(2)}) collective-permute-start(f32[136,256]{1,0:T(8,128)S(1)} %get-tuple-element.16), channel_id=1, source_target_pairs={{0,32},{32,0},{64,96},{96,64},{1,33},{33,1},{65,97},{97,65},{2,34}... | collective-permute-start | bytes 417800 | tf_op jit(solution)/shard_map/ppermute | solution.py:486
  70.8 2.6 %collective-permute-start.2 = (f32[136,256]{1,0:T(8,128)S(1)}, f32[136,256]{1,0:T(8,128)S(1)}, u32[]{:S(2)}, u32[]{:S(2)}) collective-permute-start(f32[136,256]{1,0:T(8,128)S(1)} %get-tuple-element.17), channel_id=1, source_target_pairs={{0,64},{32,96},{64,0},{96,32},{1,65},{33,97},{65,1},{97,33},{2,66}... | collective-permute-start | bytes 417800 | tf_op jit(solution)/shard_map/ppermute | solution.py:486
  73.4 0.0 collective-permute-start.3
  73.4 0.9 %collective-permute-done.1 = f32[136,256]{1,0:T(8,128)S(1)} collective-permute-done((f32[136,256]{1,0:T(8,128)S(1)}, f32[136,256]{1,0:T(8,128)S(1)}, u32[]{:S(2)}, u32[]{:S(2)}) %collective-permute-start.1) | collective-permute-done | bytes 139296 | tf_op jit(solution)/shard_map/ppermute | solution.py:486
  74.3 5.5 %collective-permute-done.2 = f32[136,256]{1,0:T(8,128)S(1)} collective-permute-done((f32[136,256]{1,0:T(8,128)S(1)}, f32[136,256]{1,0:T(8,128)S(1)}, u32[]{:S(2)}, u32[]{:S(2)}) %collective-permute-start.2) | collective-permute-done | bytes 139296 | tf_op jit(solution)/shard_map/ppermute | solution.py:486
  79.8 2.5 %collective-permute-done.3 = f32[136,256]{1,0:T(8,128)S(1)} collective-permute-done((f32[136,256]{1,0:T(8,128)S(1)}, f32[136,256]{1,0:T(8,128)S(1)}, u32[]{:S(2)}, u32[]{:S(2)}) %collective-permute-start.3) | collective-permute-done | bytes 139296 | tf_op jit(solution)/shard_map/ppermute | solution.py:486
  82.4 0.0 copy-start
  82.6 1.0 %fusion.15 = f32[128,256]{1,0:T(8,128)} fusion(f32[136,256]{1,0:T(8,128)S(1)} %get-tuple-element.2, f32[4,2048]{1,0:T(4,128)S(1)} %maximum_subtract_fusion.4, s32[]{:T(128)S(6)} %select_n.91, s32[]{:T(128)S(6)} %select_n.96), kind=kOutput, calls=%fused_computation.32 | convolution fusion | flops 1671168 | bytes 268296 | tf_op jit(solution)/shard_map/gf,gc->fc/dot_general | solution.py:491
  83.6 0.0 copy-done
  (24 shorter events, 0.5 us)
Async XLA Ops:
  37.8 24.1 %all-to-all-start = ((f32[16,16,1024]{2,1,0:T(8,128)}), f32[16,16,1024]{2,1,0:T(8,128)S(1)}, u32[]{:S(2)}, u32[]{:S(2)}) async-start(f32[16,16,1024]{2,1,0:T(8,128)} %network.1), calls=%async_computation | async-start | bytes 2097152 | tf_op jit(solution)/shard_map/all_to_all | solution.py:445
  62.2 5.1 %collective-permute-start = (f32[272,768]{1,0:T(8,128)S(1)}, f32[272,768]{1,0:T(8,128)S(1)}, u32[]{:S(2)}, u32[]{:S(2)}) collective-permute-start(f32[272,768]{1,0:T(8,128)S(1)} %select_maximum_fusion), channel_id=1, source_target_pairs={{0,1},{1,0},{2,3},{3,2},{4,5},{5,4},{6,7},{7,6},{8,9},{9,8},{10,11... | collective-permute-start | bytes 2506760 | tf_op jit(solution)/shard_map/ppermute | solution.py:461
  69.4 4.9 %collective-permute-start.1 = (f32[136,256]{1,0:T(8,128)S(1)}, f32[136,256]{1,0:T(8,128)S(1)}, u32[]{:S(2)}, u32[]{:S(2)}) collective-permute-start(f32[136,256]{1,0:T(8,128)S(1)} %get-tuple-element.16), channel_id=1, source_target_pairs={{0,32},{32,0},{64,96},{96,64},{1,33},{33,1},{65,97},{97,65},{2,34}... | collective-permute-start | bytes 417800 | tf_op jit(solution)/shard_map/ppermute | solution.py:486
  70.8 9.0 %collective-permute-start.2 = (f32[136,256]{1,0:T(8,128)S(1)}, f32[136,256]{1,0:T(8,128)S(1)}, u32[]{:S(2)}, u32[]{:S(2)}) collective-permute-start(f32[136,256]{1,0:T(8,128)S(1)} %get-tuple-element.17), channel_id=1, source_target_pairs={{0,64},{32,96},{64,0},{96,32},{1,65},{33,97},{65,1},{97,33},{2,66}... | collective-permute-start | bytes 417800 | tf_op jit(solution)/shard_map/ppermute | solution.py:486
  73.4 8.9 %collective-permute-start.3 = (f32[136,256]{1,0:T(8,128)S(1)}, f32[136,256]{1,0:T(8,128)S(1)}, u32[]{:S(2)}, u32[]{:S(2)}) collective-permute-start(f32[136,256]{1,0:T(8,128)S(1)} %get-tuple-element.15), channel_id=1, source_target_pairs={{0,96},{32,64},{64,32},{96,0},{1,97},{33,65},{65,33},{97,1},{2,98}... | collective-permute-start | bytes 417800 | tf_op jit(solution)/shard_map/ppermute | solution.py:486
  82.4 1.2 %copy-start = (f32[1,2,8,128]{3,1,2,0:T(2,128)}, f32[1,2,8,128]{3,1,2,0:T(2,128)S(1)}, u32[]{:S(2)}) copy-start(f32[1,2,8,128]{3,1,2,0:T(2,128)S(1)} %copy.15) | copy-start | bytes 24580

commit v5 on v4

--- a/solution.py
+++ b/solution.py
@@ -482,10 +482,10 @@
     )
     exchanged = [lax.dynamic_index_in_dim(parts, y, 0, False)]
     for n in (1, 3, 2):
-        part = lax.dynamic_index_in_dim(parts, y ^ n, 0, False)
-        exchanged.append(lax.ppermute(part, "y", [(k, k ^ n) for k in range(4)]))
-    own, near, wrap, far = exchanged
-    total = (own + near) + (far + wrap)
+        part = lax.dynamic_index_in_dim(parts, (y + n) % 4, 0, False)
+        exchanged.append(lax.ppermute(part, "y", [(k, (k + n) % 4) for k in range(4)]))
+    own, before, after, across = exchanged
+    total = (own + across) + (before + after)
     feature_mean = total[128:].reshape(FEAT) / 4
     gap = jnp.stack([part[128:].reshape(FEAT) for part in exchanged]) - feature_mean
     between = jnp.einsum(

time: 83.8 us -> 80.8 us (0.964)
  waiting for transfers between devices: 26.5 us -> 21.8 us
  starting transfers between devices: 15.6 us -> 17.2 us
    ppermute x3, waiting for transfers between devices: 8.94 us -> 4.27 us  [statistics(): lax.ppermute(part, 'y', [(k, (k + n) % 4) for k in range(4)])]
    ppermute x3, starting transfers between devices: 4.01 us -> 5.68 us  [statistics(): lax.ppermute(part, 'y', [(k, (k + n) % 4) for k in range(4)])]
  transfers between devices with their start and end apart: 5 -> 5, of which waited for: 5 -> 4; matrix products, arithmetic and copies ran while one was open for 0% -> 0% of each run, Pallas kernels for 0% -> 0%
where the time goes in v5:
time: 80.8 us; the launch traced here: 80.6 us
  Pallas kernels  37.2 us (46%)
  waiting for transfers between devices  21.8 us (27%)
  starting transfers between devices  17.2 us (21%)
  matrix products  2.82 us (3%)
  between operations  0.87 us (1%)
    pallas_call x1, Pallas kernels, network(): pl.pallas_call(network_kernel, out_shape=jax.ShapeDtypeStruct((16, LOCAL,...  37.2 us
    all_to_all x1, waiting for transfers between devices, statistics(): got = lax.all_to_all(message, ('xh', 'xl', 'z'), 0, 0, tiled=True)  15.6 us
    all_to_all x1, starting transfers between devices, statistics(): got = lax.all_to_all(message, ('xh', 'xl', 'z'), 0, 0, tiled=True)  8.43 us
    ppermute x3, starting transfers between devices, statistics(): lax.ppermute(part, 'y', [(k, (k + n) % 4) for k in range(4)])  5.68 us
    ppermute x3, waiting for transfers between devices, statistics(): lax.ppermute(part, 'y', [(k, (k + n) % 4) for k in range(4)])  4.27 us
    ppermute x1, starting transfers between devices, statistics(): passed = lax.ppermute(pass_on, 'core', [(0, 1), (1, 0)])  3.12 us
    ppermute x1, waiting for transfers between devices, statistics(): passed = lax.ppermute(pass_on, 'core', [(0, 1), (1, 0)])  1.94 us
    dot_general x1, matrix products, statistics(): jnp.einsum('nf,nc->fc', centered_rows, centered_columns, precision=highes...  1.82 us
  transfers between devices with their start and end apart: 5, of which 4 were waited for; matrix products, arithmetic and copies ran while one was open for 0% of the time, Pallas kernels for 0%

profile of v5, /device:TPU:1, one launch (start us, length us, event | category | flops | bytes accessed | tf_op | source)
XLA Modules:
  0.0 80.6 jit_solution(5030033656631191928)
XLA Ops:
  0.6 37.2 %network.1 = f32[16,16,1024]{2,1,0:T(8,128)} custom-call(bf16[17,17,16,768]{3,2,1,0:T(8,128)(2,1)} %bitcast.64, bf16[768,384]{1,0:T(8,128)(2,1)} %bitcast.75, bf16[1728,320]{1,0:T(8,128)(2,1)} %bitcast.67, bf16[1344,192]{1,0:T(8,128)(2,1)} %bitcast.73, bf16[1344,192]{1,0:T(8,128)(2,1)} %bitcast.74, bf16[1728,192]{1,0:T(8,128)(2,1)} %bitcast.68, ...), custom_call_target="tpu_custom_call" | custom-call | flops 19599998976 | bytes 21000000 | tf_op jit(solution)/shard_map/network/pallas_call | solution.py:402
  37.8 8.4 %all-to-all-start = ((f32[16,16,1024]{2,1,0:T(8,128)}), f32[16,16,1024]{2,1,0:T(8,128)S(1)}, u32[]{:S(2)}, u32[]{:S(2)}) async-start(f32[16,16,1024]{2,1,0:T(8,128)} %network.1), calls=%async_computation | async-start | bytes 2097152 | tf_op jit(solution)/shard_map/all_to_all | solution.py:445
  46.3 15.6 %all-to-all-done = f32[16,16,1024]{2,1,0:T(8,128)S(1)} async-done(((f32[16,16,1024]{2,1,0:T(8,128)}), f32[16,16,1024]{2,1,0:T(8,128)S(1)}, u32[]{:S(2)}, u32[]{:S(2)}) %all-to-all-start) | async-done | bytes 1048608 | tf_op jit(solution)/shard_map/all_to_all | solution.py:445
  62.1 0.1 select_maximum_fusion
  62.2 3.1 %collective-permute-start = (f32[272,768]{1,0:T(8,128)S(1)}, f32[272,768]{1,0:T(8,128)S(1)}, u32[]{:S(2)}, u32[]{:S(2)}) collective-permute-start(f32[272,768]{1,0:T(8,128)S(1)} %select_maximum_fusion), channel_id=1, source_target_pairs={{0,1},{1,0},{2,3},{3,2},{4,5},{5,4},{6,7},{7,6},{8,9},{9,8},{10,11... | collective-permute-start | bytes 2506760 | tf_op jit(solution)/shard_map/ppermute | solution.py:461
  65.4 1.9 %collective-permute-done = f32[272,768]{1,0:T(8,128)S(1)} collective-permute-done((f32[272,768]{1,0:T(8,128)S(1)}, f32[272,768]{1,0:T(8,128)S(1)}, u32[]{:S(2)}, u32[]{:S(2)}) %collective-permute-start) | collective-permute-done | bytes 835616 | tf_op jit(solution)/shard_map/ppermute | solution.py:461
  67.3 0.1 dynamic_slice.39
  67.4 0.1 slice.57
  67.5 1.8 %fusion = f32[512,256]{1,0:T(8,128)S(1)} fusion(f32[256,512]{1,0:T(8,128)S(1)} %slice.57, f32[256,512]{1,0:T(8,128)S(1)} %bitcast.52, f32[256,256]{1,0:T(8,128)S(1)} %slice.59, f32[256,256]{1,0:T(8,128)S(1)} %bitcast.54, f32[512]{0:T(512)S(1)} %bitcast.63, f32[256]{0:T(256)S(1)} %dynamic_slice.39), kind=kOutput, calls=%fused_computation.6 | convolution fusion | flops 806092800 | bytes 2100224 | tf_op jit(solution)/shard_map/nf,nc->fc/dot_general | solution.py:469
  69.4 3.0 %collective-permute-start.1 = (f32[136,256]{1,0:T(8,128)S(1)}, f32[136,256]{1,0:T(8,128)S(1)}, u32[]{:S(2)}, u32[]{:S(2)}) collective-permute-start(f32[136,256]{1,0:T(8,128)S(1)} %get-tuple-element.16), channel_id=1, source_target_pairs={{0,64},{32,96},{64,0},{96,32},{1,65},{33,97},{65,1},{97,33},{2,66}... | collective-permute-start | bytes 417800 | tf_op jit(solution)/shard_map/ppermute | solution.py:486
  72.4 0.4 collective-permute-start.2
  72.8 2.3 %collective-permute-start.3 = (f32[136,256]{1,0:T(8,128)S(1)}, f32[136,256]{1,0:T(8,128)S(1)}, u32[]{:S(2)}, u32[]{:S(2)}) collective-permute-start(f32[136,256]{1,0:T(8,128)S(1)} %get-tuple-element.15), channel_id=1, source_target_pairs={{0,96},{32,0},{64,32},{96,64},{1,97},{33,1},{65,33},{97,65},{2,98}... | collective-permute-start | bytes 417800 | tf_op jit(solution)/shard_map/ppermute | solution.py:486
  75.1 0.8 collective-permute-done.1
  75.8 3.5 %collective-permute-done.2 = f32[136,256]{1,0:T(8,128)S(1)} collective-permute-done((f32[136,256]{1,0:T(8,128)S(1)}, f32[136,256]{1,0:T(8,128)S(1)}, u32[]{:S(2)}, u32[]{:S(2)}) %collective-permute-start.2) | collective-permute-done | bytes 139296 | tf_op jit(solution)/shard_map/ppermute | solution.py:486
  79.3 0.0 collective-permute-done.3
  79.4 0.0 copy-start
  79.6 1.0 %fusion.15 = f32[128,256]{1,0:T(8,128)} fusion(f32[136,256]{1,0:T(8,128)S(1)} %get-tuple-element.2, f32[4,2048]{1,0:T(4,128)S(1)} %maximum_subtract_fusion.4, s32[]{:T(128)S(6)} %select_n.106, s32[]{:T(128)S(6)} %select_n.114), kind=kOutput, calls=%fused_computation.32 | convolution fusion | flops 1671168 | bytes 268296 | tf_op jit(solution)/shard_map/gf,gc->fc/dot_general | solution.py:491
  80.6 0.0 copy-done
  (24 shorter events, 0.5 us)
Async XLA Ops:
  37.8 24.1 %all-to-all-start = ((f32[16,16,1024]{2,1,0:T(8,128)}), f32[16,16,1024]{2,1,0:T(8,128)S(1)}, u32[]{:S(2)}, u32[]{:S(2)}) async-start(f32[16,16,1024]{2,1,0:T(8,128)} %network.1), calls=%async_computation | async-start | bytes 2097152 | tf_op jit(solution)/shard_map/all_to_all | solution.py:445
  62.2 5.1 %collective-permute-start = (f32[272,768]{1,0:T(8,128)S(1)}, f32[272,768]{1,0:T(8,128)S(1)}, u32[]{:S(2)}, u32[]{:S(2)}) collective-permute-start(f32[272,768]{1,0:T(8,128)S(1)} %select_maximum_fusion), channel_id=1, source_target_pairs={{0,1},{1,0},{2,3},{3,2},{4,5},{5,4},{6,7},{7,6},{8,9},{9,8},{10,11... | collective-permute-start | bytes 2506760 | tf_op jit(solution)/shard_map/ppermute | solution.py:461
  69.4 6.4 %collective-permute-start.1 = (f32[136,256]{1,0:T(8,128)S(1)}, f32[136,256]{1,0:T(8,128)S(1)}, u32[]{:S(2)}, u32[]{:S(2)}) collective-permute-start(f32[136,256]{1,0:T(8,128)S(1)} %get-tuple-element.16), channel_id=1, source_target_pairs={{0,64},{32,96},{64,0},{96,32},{1,65},{33,97},{65,1},{97,33},{2,66}... | collective-permute-start | bytes 417800 | tf_op jit(solution)/shard_map/ppermute | solution.py:486
  72.4 6.9 %collective-permute-start.2 = (f32[136,256]{1,0:T(8,128)S(1)}, f32[136,256]{1,0:T(8,128)S(1)}, u32[]{:S(2)}, u32[]{:S(2)}) collective-permute-start(f32[136,256]{1,0:T(8,128)S(1)} %get-tuple-element.17), channel_id=1, source_target_pairs={{0,32},{32,64},{64,96},{96,0},{1,33},{33,65},{65,97},{97,1},{2,34}... | collective-permute-start | bytes 417800 | tf_op jit(solution)/shard_map/ppermute | solution.py:486
  72.8 6.5 %collective-permute-start.3 = (f32[136,256]{1,0:T(8,128)S(1)}, f32[136,256]{1,0:T(8,128)S(1)}, u32[]{:S(2)}, u32[]{:S(2)}) collective-permute-start(f32[136,256]{1,0:T(8,128)S(1)} %get-tuple-element.15), channel_id=1, source_target_pairs={{0,96},{32,0},{64,32},{96,64},{1,97},{33,1},{65,33},{97,65},{2,98}... | collective-permute-start | bytes 417800 | tf_op jit(solution)/shard_map/ppermute | solution.py:486
  79.4 1.2 %copy-start = (f32[1,2,8,128]{3,1,2,0:T(2,128)}, f32[1,2,8,128]{3,1,2,0:T(2,128)S(1)}, u32[]{:S(2)}) copy-start(f32[1,2,8,128]{3,1,2,0:T(2,128)S(1)} %copy.15) | copy-start | bytes 24580

commit v6 on v5

--- a/solution.py
+++ b/solution.py
@@ -108,14 +108,14 @@
 
     moves = {"entry": (entry_hbm, entry_w, 0)}
     copy("entry").start()
-    def x_third(i, first):
-        source = x_hbm.at[pl.ds(8 * i + first, 3)]
-        target = x.at[pl.ds(9 * i + first, 3)]
-        return pltpu.make_async_copy(source, target, sems.at[1 + 3 * i + first // 3])
-
-    for i in range(2):
-        for first in (0, 3, 6):
-            x_third(i, first).start()
+    thirds = [(0, 3), (3, 3), (6, 3), (9, 3), (12, 3), (15, 2)]
+
+    def x_rows(first, count):
+        source, target = x_hbm.at[pl.ds(first, count)], x.at[pl.ds(first, count)]
+        return pltpu.make_async_copy(source, target, sems.at[1 + first // 3])
+
+    for first, count in thirds:
+        x_rows(first, count).start()
 
     def start_later():
         for name, _, _ in later:
@@ -136,6 +136,7 @@
     ]
     for i, (name, source, target) in enumerate(later):
         moves[name] = (source, target, 7 + i)
+    start_later()
 
     deep_last[...] = jnp.zeros((10, 10, LOCAL, 128), BF)
     deep_first[...] = jnp.zeros((10, 10, LOCAL, 128), BF)
@@ -153,7 +154,7 @@
         array[1:9, 9] = jnp.zeros((8, LOCAL, channels), BF)
 
     def split_by_parity(i, first, values, head, ends, tail):
-        for r in range(first, first + 3):
+        for r in range(first, first + values.shape[0]):
             for c in range(17):
                 at = (r % 2, c % 2, 4 * i + r // 2, c // 2)
                 place = values[r - first, c]
@@ -162,45 +163,35 @@
                 ends[(*at, slice(None), slice(64, 128))] = place[:, 0:64]
                 tail[at] = place[:, 64:192]
 
-    def in_thirds(product, keep):
-        earlier = product(0)
-        for first in (3, 6):
-            latter = product(first)
-            keep(first - 3, earlier)
-            earlier = latter
-        keep(6, earlier)
-
     copy("entry").wait()
 
-    def entry_block(i, carry):
-        @pl.when(i == 1)
-        def _():
-            start_later()
-
-        def product(first):
-            x_third(i, first).wait()
-            return dot(x[pl.ds(9 * i + first, 3)].reshape(816, 768), entry_w[...])
-
-        def keep(first, values):
-            values = relu(values).reshape(3, 17, LOCAL, 384)
-            rows = pl.ds(8 * i + first, 3)
-            long_head[rows, 3:20] = values[..., 192:320]
-            long_joint[rows, 3:20, :, 0:64] = values[..., 320:384]
-            long_joint[rows, 2:19, :, 64:128] = values[..., 192:256]
-            long_tail[rows, 3:20] = values[..., 256:384]
-            split_by_parity(i, first, values, short_head, short_ends, short_tail)
-
-        in_thirds(product, keep)
-        return carry
-
-    lax.fori_loop(0, 2, entry_block, 0)
+    def entry_product(first, count):
+        x_rows(first, count).wait()
+        return dot(x[first : first + count].reshape(count * 272, 768), entry_w[...])
+
+    def keep_entry(first, count, values):
+        values = relu(values).reshape(count, 17, LOCAL, 384)
+        rows = slice(first, first + count)
+        long_head[rows, 3:20] = values[..., 192:320]
+        long_joint[rows, 3:20, :, 0:64] = values[..., 320:384]
+        long_joint[rows, 2:19, :, 64:128] = values[..., 192:256]
+        long_tail[rows, 3:20] = values[..., 256:384]
+        split_by_parity(0, first, values, short_head, short_ends, short_tail)
+
+    earlier = None
+    for first, count in thirds:
+        latter = entry_product(first, count)
+        if earlier is not None:
+            keep_entry(*earlier)
+        earlier = (first, count, latter)
+    keep_entry(*earlier)
 
     copy("row").wait()
 
     def maximum(i, r):
         tall = [
             jnp.maximum(
-                jnp.maximum(x[9 * i + 2 * r, c], x[9 * i + 2 * r + 1, c]), x[9 * i + 2 * r + 2, c]
+                jnp.maximum(x[8 * i + 2 * r, c], x[8 * i + 2 * r + 1, c]), x[8 * i + 2 * r + 2, c]
             )
             for c in range(17)
         ]
@@ -209,9 +200,9 @@
                 jnp.maximum(tall[2 * c], tall[2 * c + 1]), tall[2 * c + 2]
             )
 
-    def row_block(i, carry):
+    def row_product(first, count, fillers):
         def at(array, t):
-            return array[pl.ds(8 * i, 9), t : t + 17].reshape(2448, 128)
+            return array[first : first + count, t : t + 17].reshape(count * 272, 128)
 
         tiles = pack(
             7,
@@ -219,20 +210,25 @@
             lambda t, u: at(long_joint, t),
             lambda t: at(long_tail, t),
         )
-        fillers = [functools.partial(maximum, i, r) for r in range(4)]
-        values = relu(contract(tiles, row_w, fillers)).reshape(9, 17, LOCAL, 192)
-        row_head[pl.ds(8 * i + 3, 9)] = values[..., 0:128]
-        row_joint[pl.ds(8 * i + 3, 9), :, :, 0:64] = values[..., 128:192]
-        row_joint[pl.ds(8 * i + 2, 9), :, :, 64:128] = values[..., 0:64]
-        row_tail[pl.ds(8 * i + 3, 9)] = values[..., 64:192]
-        return carry
-
-    lax.fori_loop(0, 2, row_block, 0)
+        return contract(tiles, row_w, fillers)
+
+    def keep_row(first, count, values):
+        values = relu(values).reshape(count, 17, LOCAL, 192)
+        row_head[first + 3 : first + 3 + count] = values[..., 0:128]
+        row_joint[first + 3 : first + 3 + count, :, :, 0:64] = values[..., 128:192]
+        row_joint[first + 2 : first + 2 + count, :, :, 64:128] = values[..., 0:64]
+        row_tail[first + 3 : first + 3 + count] = values[..., 64:192]
+
+    fillers = [functools.partial(maximum, r // 4, r % 4) for r in range(8)]
+    upper = row_product(0, 9, fillers[:4])
+    lower_rows = row_product(9, 8, fillers[4:])
+    keep_row(0, 9, upper)
+    keep_row(9, 8, lower_rows)
     copy("column").wait()
 
-    def column_block(i, carry):
+    def column_product(first, count):
         def at(array, t):
-            return array[pl.ds(8 * i + t, 9)].reshape(2448, 128)
+            return array[first + t : first + t + count].reshape(count * 272, 128)
 
         tiles = pack(
             7,
@@ -240,14 +236,16 @@
             lambda t, u: at(row_joint, t),
             lambda t: at(row_tail, t),
         )
-        values = relu(contract(tiles, column_w)).reshape(9, 17, LOCAL, 192)
-        for first in (0, 3, 6):
-            split_by_parity(
-                i, first, values[first : first + 3], tower_head, tower_ends, tower_tail
-            )
-        return carry
-
-    lax.fori_loop(0, 2, column_block, 0)
+        return contract(tiles, column_w)
+
+    def keep_column(first, count, values):
+        values = relu(values).reshape(count, 17, LOCAL, 192)
+        split_by_parity(0, first, values, tower_head, tower_ends, tower_tail)
+
+    upper = column_product(0, 9)
+    lower_rows = column_product(9, 8)
+    keep_column(0, 9, upper)
+    keep_column(9, 8, lower_rows)
     copy("wide").wait()
     copy("reduce").wait()
 
@@ -269,9 +267,9 @@
         return relu(contract(pack(9, head, functools.partial(joined, ends), tail), weights))
 
     def reduce_block(i):
+        tower_out = strided((tower_head, tower_ends, tower_tail), reduce_w, i)
         wide_out = strided((short_head, short_ends, short_tail), wide_w, i)
         middle[pl.ds(i + 1, 4), 1:9, :, 0:320] = wide_out.reshape(4, 8, LOCAL, 320)
-        tower_out = strided((tower_head, tower_ends, tower_tail), reduce_w, i)
         middle[pl.ds(i + 1, 4), 1:9, :, 320:512] = tower_out.reshape(4, 8, LOCAL, 192)
 
     half_map(reduce_block)
@@ -283,9 +281,11 @@
 
     copy("second").wait()
 
-    def second_block(i):
-        flat = middle[pl.ds(i + 1, 4), 1:9].reshape(512, 1280)
-        second = relu(dot(flat, second_w[...]))
+    def second_product(i):
+        return dot(middle[i + 1 : i + 5, 1:9].reshape(512, 1280), second_w[...])
+
+    def keep_second(i, values):
+        second = relu(values)
         add_sums(i, 0, second[:, 0:320])
         rows = pl.ds(i + 1, 4)
         branch[0, rows, 1:9] = second[:, 320:704].reshape(4, 8, LOCAL, 384)
@@ -294,7 +294,9 @@
         deep_first[rows, 1:9, :, 64:128] = second[:, 704:768].reshape(4, 8, LOCAL, 64)
         deep_tail[rows, 1:9] = second[:, 768:1152].reshape(4, 8, LOCAL, 384)
 
-    half_map(second_block)
+    upper, lower_half = second_product(0), second_product(4)
+    keep_second(0, upper)
+    keep_second(4, lower_half)
 
     copy("second_deep").wait()
     copy("pool").wait()
@@ -340,16 +342,24 @@
     for name in ("second_row", "second_column", "deep_row", "deep_column"):
         copy(name).wait()
 
-    def branch_map(n, carry):
-        def tap(t):
-            down, right = jnp.where(n % 2 == 0, 1, t), jnp.where(n % 2 == 0, t, 1)
-            return branch[n // 2, pl.ds(down, 8), pl.ds(right, 8)].reshape(1024, 384)
-
-        values = relu(dot(jnp.concatenate([tap(t) for t in range(3)], axis=1), branch_w[n]))
-        branch_sums[n] = jnp.sum(values.astype(F32).reshape(64, LOCAL, 384), axis=0)
+    def branch_pair(n, carry):
+        def tap(down, right):
+            return branch[n, pl.ds(down, 8), pl.ds(right, 8)].reshape(1024, 384)
+
+        def product(taps, kind):
+            return dot(jnp.concatenate(taps, axis=1), branch_w[2 * n + kind])
+
+        def keep(values, kind):
+            values = relu(values).astype(F32).reshape(64, LOCAL, 384)
+            branch_sums[2 * n + kind] = jnp.sum(values, axis=0)
+
+        across = product([tap(1, t) for t in range(3)], 0)
+        down = product([tap(t, 1) for t in range(3)], 1)
+        keep(across, 0)
+        keep(down, 1)
         return carry
 
-    lax.fori_loop(0, 4, branch_map, 0)
+    lax.fori_loop(0, 2, branch_pair, 0)
     for n in range(4):
         features[:, 320 + 384 * n : 704 + 384 * n] = branch_sums[n]
     for block in range(16):
@@ -404,7 +414,7 @@
         out_shape=jax.ShapeDtypeStruct((16, LOCAL, 1024), F32),
         in_specs=[pl.BlockSpec(memory_space=pl.ANY)] * 13,
         out_specs=pl.BlockSpec(memory_space=pltpu.VMEM),
-        scratch_shapes=[place(18, 17, LOCAL, 768)]
+        scratch_shapes=[place(17, 17, LOCAL, 768)]
         + [place(*a.shape) for a in operands[1:7]]
         + [place(4032, 384), place(4, 1152, 384), place(192, 1280)]
         + [place(17, 23, LOCAL, 128)] * 3

time: 80.8 us -> 78.8 us (0.975)
  Pallas kernels: 37.2 us -> 35.2 us
    pallas_call x1, Pallas kernels: 37.2 us -> 35.2 us  [network(): pl.pallas_call(network_kernel, out_shape=jax.ShapeDtypeStruct((16, LOCAL,...]
where the time goes in v6:
time: 78.8 us; the launch traced here: 78.7 us
  Pallas kernels  35.2 us (45%)
  waiting for transfers between devices  21.9 us (28%)
  starting transfers between devices  17.2 us (22%)
  matrix products  2.82 us (4%)
  between operations  0.87 us (1%)
    pallas_call x1, Pallas kernels, network(): pl.pallas_call(network_kernel, out_shape=jax.ShapeDtypeStruct((16, LOCAL,...  35.2 us
    all_to_all x1, waiting for transfers between devices, statistics(): got = lax.all_to_all(message, ('xh', 'xl', 'z'), 0, 0, tiled=True)  15.6 us
    all_to_all x1, starting transfers between devices, statistics(): got = lax.all_to_all(message, ('xh', 'xl', 'z'), 0, 0, tiled=True)  8.44 us
    ppermute x3, starting transfers between devices, statistics(): lax.ppermute(part, 'y', [(k, (k + n) % 4) for k in range(4)])  5.66 us
    ppermute x3, waiting for transfers between devices, statistics(): lax.ppermute(part, 'y', [(k, (k + n) % 4) for k in range(4)])  4.28 us
    ppermute x1, starting transfers between devices, statistics(): passed = lax.ppermute(pass_on, 'core', [(0, 1), (1, 0)])  3.11 us
    ppermute x1, waiting for transfers between devices, statistics(): passed = lax.ppermute(pass_on, 'core', [(0, 1), (1, 0)])  1.94 us
    dot_general x1, matrix products, statistics(): jnp.einsum('nf,nc->fc', centered_rows, centered_columns, precision=highes...  1.82 us
  transfers between devices with their start and end apart: 5, of which 4 were waited for; matrix products, arithmetic and copies ran while one was open for 0% of the time, Pallas kernels for 0%

profile of v6, /device:TPU:1, one launch (start us, length us, event | category | flops | bytes accessed | tf_op | source)
XLA Modules:
  0.0 78.7 jit_solution(14453920231245014875)
XLA Ops:
  0.6 35.2 %network.1 = f32[16,16,1024]{2,1,0:T(8,128)} custom-call(bf16[17,17,16,768]{3,2,1,0:T(8,128)(2,1)} %bitcast.64, bf16[768,384]{1,0:T(8,128)(2,1)} %bitcast.75, bf16[1728,320]{1,0:T(8,128)(2,1)} %bitcast.67, bf16[1344,192]{1,0:T(8,128)(2,1)} %bitcast.73, bf16[1344,192]{1,0:T(8,128)(2,1)} %bitcast.74, bf16[1728,192]{1,0:T(8,128)(2,1)} %bitcast.68, ...), custom_call_target="tpu_custom_call" | custom-call | flops 19599998976 | bytes 21000000 | tf_op jit(solution)/shard_map/network/pallas_call | solution.py:412
  35.9 8.4 %all-to-all-start = ((f32[16,16,1024]{2,1,0:T(8,128)}), f32[16,16,1024]{2,1,0:T(8,128)S(1)}, u32[]{:S(2)}, u32[]{:S(2)}) async-start(f32[16,16,1024]{2,1,0:T(8,128)} %network.1), calls=%async_computation | async-start | bytes 2097152 | tf_op jit(solution)/shard_map/all_to_all | solution.py:455
  44.4 15.6 %all-to-all-done = f32[16,16,1024]{2,1,0:T(8,128)S(1)} async-done(((f32[16,16,1024]{2,1,0:T(8,128)}), f32[16,16,1024]{2,1,0:T(8,128)S(1)}, u32[]{:S(2)}, u32[]{:S(2)}) %all-to-all-start) | async-done | bytes 1048608 | tf_op jit(solution)/shard_map/all_to_all | solution.py:455
  60.2 0.1 select_maximum_fusion
  60.3 3.1 %collective-permute-start = (f32[272,768]{1,0:T(8,128)S(1)}, f32[272,768]{1,0:T(8,128)S(1)}, u32[]{:S(2)}, u32[]{:S(2)}) collective-permute-start(f32[272,768]{1,0:T(8,128)S(1)} %select_maximum_fusion), channel_id=1, source_target_pairs={{0,1},{1,0},{2,3},{3,2},{4,5},{5,4},{6,7},{7,6},{8,9},{9,8},{10,11... | collective-permute-start | bytes 2506760 | tf_op jit(solution)/shard_map/ppermute | solution.py:471
  63.5 1.9 %collective-permute-done = f32[272,768]{1,0:T(8,128)S(1)} collective-permute-done((f32[272,768]{1,0:T(8,128)S(1)}, f32[272,768]{1,0:T(8,128)S(1)}, u32[]{:S(2)}, u32[]{:S(2)}) %collective-permute-start) | collective-permute-done | bytes 835616 | tf_op jit(solution)/shard_map/ppermute | solution.py:471
  65.4 0.1 dynamic_slice.39
  65.5 0.1 slice.57
  65.6 1.8 %fusion = f32[512,256]{1,0:T(8,128)S(1)} fusion(f32[256,512]{1,0:T(8,128)S(1)} %slice.57, f32[256,512]{1,0:T(8,128)S(1)} %bitcast.52, f32[256,256]{1,0:T(8,128)S(1)} %slice.59, f32[256,256]{1,0:T(8,128)S(1)} %bitcast.54, f32[512]{0:T(512)S(1)} %bitcast.63, f32[256]{0:T(256)S(1)} %dynamic_slice.39), kind=kOutput, calls=%fused_computation.6 | convolution fusion | flops 806092800 | bytes 2100224 | tf_op jit(solution)/shard_map/nf,nc->fc/dot_general | solution.py:479
  67.5 3.0 %collective-permute-start.1 = (f32[136,256]{1,0:T(8,128)S(1)}, f32[136,256]{1,0:T(8,128)S(1)}, u32[]{:S(2)}, u32[]{:S(2)}) collective-permute-start(f32[136,256]{1,0:T(8,128)S(1)} %get-tuple-element.16), channel_id=1, source_target_pairs={{0,64},{32,96},{64,0},{96,32},{1,65},{33,97},{65,1},{97,33},{2,66}... | collective-permute-start | bytes 417800 | tf_op jit(solution)/shard_map/ppermute | solution.py:496
  70.5 0.4 collective-permute-start.2
  70.8 2.3 %collective-permute-start.3 = (f32[136,256]{1,0:T(8,128)S(1)}, f32[136,256]{1,0:T(8,128)S(1)}, u32[]{:S(2)}, u32[]{:S(2)}) collective-permute-start(f32[136,256]{1,0:T(8,128)S(1)} %get-tuple-element.15), channel_id=1, source_target_pairs={{0,96},{32,0},{64,32},{96,64},{1,97},{33,1},{65,33},{97,65},{2,98}... | collective-permute-start | bytes 417800 | tf_op jit(solution)/shard_map/ppermute | solution.py:496
  73.1 0.8 collective-permute-done.1
  73.9 3.5 %collective-permute-done.2 = f32[136,256]{1,0:T(8,128)S(1)} collective-permute-done((f32[136,256]{1,0:T(8,128)S(1)}, f32[136,256]{1,0:T(8,128)S(1)}, u32[]{:S(2)}, u32[]{:S(2)}) %collective-permute-start.2) | collective-permute-done | bytes 139296 | tf_op jit(solution)/shard_map/ppermute | solution.py:496
  77.4 0.0 collective-permute-done.3
  77.5 0.0 copy-start
  77.7 1.0 %fusion.15 = f32[128,256]{1,0:T(8,128)} fusion(f32[136,256]{1,0:T(8,128)S(1)} %get-tuple-element.2, f32[4,2048]{1,0:T(4,128)S(1)} %maximum_subtract_fusion.4, s32[]{:T(128)S(6)} %select_n.106, s32[]{:T(128)S(6)} %select_n.114), kind=kOutput, calls=%fused_computation.32 | convolution fusion | flops 1671168 | bytes 268296 | tf_op jit(solution)/shard_map/gf,gc->fc/dot_general | solution.py:501
  78.7 0.0 copy-done
  (24 shorter events, 0.5 us)
Async XLA Ops:
  35.9 24.1 %all-to-all-start = ((f32[16,16,1024]{2,1,0:T(8,128)}), f32[16,16,1024]{2,1,0:T(8,128)S(1)}, u32[]{:S(2)}, u32[]{:S(2)}) async-start(f32[16,16,1024]{2,1,0:T(8,128)} %network.1), calls=%async_computation | async-start | bytes 2097152 | tf_op jit(solution)/shard_map/all_to_all | solution.py:455
  60.3 5.1 %collective-permute-start = (f32[272,768]{1,0:T(8,128)S(1)}, f32[272,768]{1,0:T(8,128)S(1)}, u32[]{:S(2)}, u32[]{:S(2)}) collective-permute-start(f32[272,768]{1,0:T(8,128)S(1)} %select_maximum_fusion), channel_id=1, source_target_pairs={{0,1},{1,0},{2,3},{3,2},{4,5},{5,4},{6,7},{7,6},{8,9},{9,8},{10,11... | collective-permute-start | bytes 2506760 | tf_op jit(solution)/shard_map/ppermute | solution.py:471
  67.5 6.4 %collective-permute-start.1 = (f32[136,256]{1,0:T(8,128)S(1)}, f32[136,256]{1,0:T(8,128)S(1)}, u32[]{:S(2)}, u32[]{:S(2)}) collective-permute-start(f32[136,256]{1,0:T(8,128)S(1)} %get-tuple-element.16), channel_id=1, source_target_pairs={{0,64},{32,96},{64,0},{96,32},{1,65},{33,97},{65,1},{97,33},{2,66}... | collective-permute-start | bytes 417800 | tf_op jit(solution)/shard_map/ppermute | solution.py:496
  70.5 7.0 %collective-permute-start.2 = (f32[136,256]{1,0:T(8,128)S(1)}, f32[136,256]{1,0:T(8,128)S(1)}, u32[]{:S(2)}, u32[]{:S(2)}) collective-permute-start(f32[136,256]{1,0:T(8,128)S(1)} %get-tuple-element.17), channel_id=1, source_target_pairs={{0,32},{32,64},{64,96},{96,0},{1,33},{33,65},{65,97},{97,1},{2,34}... | collective-permute-start | bytes 417800 | tf_op jit(solution)/shard_map/ppermute | solution.py:496
  70.8 6.6 %collective-permute-start.3 = (f32[136,256]{1,0:T(8,128)S(1)}, f32[136,256]{1,0:T(8,128)S(1)}, u32[]{:S(2)}, u32[]{:S(2)}) collective-permute-start(f32[136,256]{1,0:T(8,128)S(1)} %get-tuple-element.15), channel_id=1, source_target_pairs={{0,96},{32,0},{64,32},{96,64},{1,97},{33,1},{65,33},{97,65},{2,98}... | collective-permute-start | bytes 417800 | tf_op jit(solution)/shard_map/ppermute | solution.py:496
  77.5 1.2 %copy-start = (f32[1,2,8,128]{3,1,2,0:T(2,128)}, f32[1,2,8,128]{3,1,2,0:T(2,128)S(1)}, u32[]{:S(2)}) copy-start(f32[1,2,8,128]{3,1,2,0:T(2,128)S(1)} %copy.15) | copy-start | bytes 24580

commit v7 on v6

--- a/solution.py
+++ b/solution.py
@@ -480,7 +480,7 @@
         "nf,nc->fc",
         centered_rows,
         centered_columns,
-        precision=highest,
+        precision=lax.Precision.HIGH,
         preferred_element_type=jnp.float32,
     )
     parts = jnp.concatenate(

time: 78.8 us -> 78 us (0.990)
  matrix products: 2.82 us -> 2.01 us
    dot_general x1, matrix products: 1.82 us -> 1.01 us  [statistics(): jnp.einsum('nf,nc->fc', centered_rows, centered_columns, precision=lax.Pr...]
where the time goes in v7:
time: 78 us; the launch traced here: 77.8 us
  Pallas kernels  35.2 us (45%)
  waiting for transfers between devices  21.9 us (28%)
  starting transfers between devices  17.2 us (22%)
  matrix products  2.01 us (3%)
  between operations  0.87 us (1%)
    pallas_call x1, Pallas kernels, network(): pl.pallas_call(network_kernel, out_shape=jax.ShapeDtypeStruct((16, LOCAL,...  35.2 us
    all_to_all x1, waiting for transfers between devices, statistics(): got = lax.all_to_all(message, ('xh', 'xl', 'z'), 0, 0, tiled=True)  15.6 us
    all_to_all x1, starting transfers between devices, statistics(): got = lax.all_to_all(message, ('xh', 'xl', 'z'), 0, 0, tiled=True)  8.44 us
    ppermute x3, starting transfers between devices, statistics(): lax.ppermute(part, 'y', [(k, (k + n) % 4) for k in range(4)])  5.66 us
    ppermute x3, waiting for transfers between devices, statistics(): lax.ppermute(part, 'y', [(k, (k + n) % 4) for k in range(4)])  4.28 us
    ppermute x1, starting transfers between devices, statistics(): passed = lax.ppermute(pass_on, 'core', [(0, 1), (1, 0)])  3.11 us
    ppermute x1, waiting for transfers between devices, statistics(): passed = lax.ppermute(pass_on, 'core', [(0, 1), (1, 0)])  1.94 us
  transfers between devices with their start and end apart: 5, of which 4 were waited for; matrix products, arithmetic and copies ran while one was open for 0% of the time, Pallas kernels for 0%

profile of v7, /device:TPU:1, one launch (start us, length us, event | category | flops | bytes accessed | tf_op | source)
XLA Modules:
  0.0 77.8 jit_solution(4355300182265305227)
XLA Ops:
  0.6 35.2 %network.1 = f32[16,16,1024]{2,1,0:T(8,128)} custom-call(bf16[17,17,16,768]{3,2,1,0:T(8,128)(2,1)} %bitcast.64, bf16[768,384]{1,0:T(8,128)(2,1)} %bitcast.75, bf16[1728,320]{1,0:T(8,128)(2,1)} %bitcast.67, bf16[1344,192]{1,0:T(8,128)(2,1)} %bitcast.73, bf16[1344,192]{1,0:T(8,128)(2,1)} %bitcast.74, bf16[1728,192]{1,0:T(8,128)(2,1)} %bitcast.68, ...), custom_call_target="tpu_custom_call" | custom-call | flops 19599998976 | bytes 21000000 | tf_op jit(solution)/shard_map/network/pallas_call | solution.py:412
  35.9 8.4 %all-to-all-start = ((f32[16,16,1024]{2,1,0:T(8,128)}), f32[16,16,1024]{2,1,0:T(8,128)S(1)}, u32[]{:S(2)}, u32[]{:S(2)}) async-start(f32[16,16,1024]{2,1,0:T(8,128)} %network.1), calls=%async_computation | async-start | bytes 2097152 | tf_op jit(solution)/shard_map/all_to_all | solution.py:455
  44.4 15.6 %all-to-all-done = f32[16,16,1024]{2,1,0:T(8,128)S(1)} async-done(((f32[16,16,1024]{2,1,0:T(8,128)}), f32[16,16,1024]{2,1,0:T(8,128)S(1)}, u32[]{:S(2)}, u32[]{:S(2)}) %all-to-all-start) | async-done | bytes 1048608 | tf_op jit(solution)/shard_map/all_to_all | solution.py:455
  60.2 0.1 select_maximum_fusion
  60.3 3.1 %collective-permute-start = (f32[272,768]{1,0:T(8,128)S(1)}, f32[272,768]{1,0:T(8,128)S(1)}, u32[]{:S(2)}, u32[]{:S(2)}) collective-permute-start(f32[272,768]{1,0:T(8,128)S(1)} %select_maximum_fusion), channel_id=1, source_target_pairs={{0,1},{1,0},{2,3},{3,2},{4,5},{5,4},{6,7},{7,6},{8,9},{9,8},{10,11... | collective-permute-start | bytes 2506760 | tf_op jit(solution)/shard_map/ppermute | solution.py:471
  63.5 1.9 %collective-permute-done = f32[272,768]{1,0:T(8,128)S(1)} collective-permute-done((f32[272,768]{1,0:T(8,128)S(1)}, f32[272,768]{1,0:T(8,128)S(1)}, u32[]{:S(2)}, u32[]{:S(2)}) %collective-permute-start) | collective-permute-done | bytes 835616 | tf_op jit(solution)/shard_map/ppermute | solution.py:471
  65.4 0.1 dynamic_slice.39
  65.5 0.1 slice.57
  65.6 1.0 %fusion = f32[512,256]{1,0:T(8,128)S(1)} fusion(f32[256,512]{1,0:T(8,128)S(1)} %slice.57, f32[256,512]{1,0:T(8,128)S(1)} %bitcast.52, f32[256,256]{1,0:T(8,128)S(1)} %slice.59, f32[256,256]{1,0:T(8,128)S(1)} %bitcast.54, f32[512]{0:T(512)S(1)} %bitcast.63, f32[256]{0:T(256)S(1)} %dynamic_slice.39), kind=kOutput, calls=%fused_computation.6 | convolution fusion | flops 403439616 | bytes 2100224 | tf_op jit(solution)/shard_map/nf,nc->fc/dot_general | solution.py:479
  66.7 3.0 %collective-permute-start.1 = (f32[136,256]{1,0:T(8,128)S(1)}, f32[136,256]{1,0:T(8,128)S(1)}, u32[]{:S(2)}, u32[]{:S(2)}) collective-permute-start(f32[136,256]{1,0:T(8,128)S(1)} %get-tuple-element.16), channel_id=1, source_target_pairs={{0,64},{32,96},{64,0},{96,32},{1,65},{33,97},{65,1},{97,33},{2,66}... | collective-permute-start | bytes 417800 | tf_op jit(solution)/shard_map/ppermute | solution.py:496
  69.6 0.4 collective-permute-start.2
  70.0 2.3 %collective-permute-start.3 = (f32[136,256]{1,0:T(8,128)S(1)}, f32[136,256]{1,0:T(8,128)S(1)}, u32[]{:S(2)}, u32[]{:S(2)}) collective-permute-start(f32[136,256]{1,0:T(8,128)S(1)} %get-tuple-element.15), channel_id=1, source_target_pairs={{0,96},{32,0},{64,32},{96,64},{1,97},{33,1},{65,33},{97,65},{2,98}... | collective-permute-start | bytes 417800 | tf_op jit(solution)/shard_map/ppermute | solution.py:496
  72.3 0.8 collective-permute-done.1
  73.1 3.5 %collective-permute-done.2 = f32[136,256]{1,0:T(8,128)S(1)} collective-permute-done((f32[136,256]{1,0:T(8,128)S(1)}, f32[136,256]{1,0:T(8,128)S(1)}, u32[]{:S(2)}, u32[]{:S(2)}) %collective-permute-start.2) | collective-permute-done | bytes 139296 | tf_op jit(solution)/shard_map/ppermute | solution.py:496
  76.6 0.0 collective-permute-done.3
  76.7 0.0 copy-start
  76.8 1.0 %fusion.15 = f32[128,256]{1,0:T(8,128)} fusion(f32[136,256]{1,0:T(8,128)S(1)} %get-tuple-element.2, f32[4,2048]{1,0:T(4,128)S(1)} %maximum_subtract_fusion.4, s32[]{:T(128)S(6)} %select_n.106, s32[]{:T(128)S(6)} %select_n.114), kind=kOutput, calls=%fused_computation.32 | convolution fusion | flops 1671168 | bytes 268296 | tf_op jit(solution)/shard_map/gf,gc->fc/dot_general | solution.py:501
  77.8 0.0 copy-done
  (24 shorter events, 0.5 us)
Async XLA Ops:
  35.9 24.1 %all-to-all-start = ((f32[16,16,1024]{2,1,0:T(8,128)}), f32[16,16,1024]{2,1,0:T(8,128)S(1)}, u32[]{:S(2)}, u32[]{:S(2)}) async-start(f32[16,16,1024]{2,1,0:T(8,128)} %network.1), calls=%async_computation | async-start | bytes 2097152 | tf_op jit(solution)/shard_map/all_to_all | solution.py:455
  60.3 5.1 %collective-permute-start = (f32[272,768]{1,0:T(8,128)S(1)}, f32[272,768]{1,0:T(8,128)S(1)}, u32[]{:S(2)}, u32[]{:S(2)}) collective-permute-start(f32[272,768]{1,0:T(8,128)S(1)} %select_maximum_fusion), channel_id=1, source_target_pairs={{0,1},{1,0},{2,3},{3,2},{4,5},{5,4},{6,7},{7,6},{8,9},{9,8},{10,11... | collective-permute-start | bytes 2506760 | tf_op jit(solution)/shard_map/ppermute | solution.py:471
  66.7 6.4 %collective-permute-start.1 = (f32[136,256]{1,0:T(8,128)S(1)}, f32[136,256]{1,0:T(8,128)S(1)}, u32[]{:S(2)}, u32[]{:S(2)}) collective-permute-start(f32[136,256]{1,0:T(8,128)S(1)} %get-tuple-element.16), channel_id=1, source_target_pairs={{0,64},{32,96},{64,0},{96,32},{1,65},{33,97},{65,1},{97,33},{2,66}... | collective-permute-start | bytes 417800 | tf_op jit(solution)/shard_map/ppermute | solution.py:496
  69.6 7.0 %collective-permute-start.2 = (f32[136,256]{1,0:T(8,128)S(1)}, f32[136,256]{1,0:T(8,128)S(1)}, u32[]{:S(2)}, u32[]{:S(2)}) collective-permute-start(f32[136,256]{1,0:T(8,128)S(1)} %get-tuple-element.17), channel_id=1, source_target_pairs={{0,32},{32,64},{64,96},{96,0},{1,33},{33,65},{65,97},{97,1},{2,34}... | collective-permute-start | bytes 417800 | tf_op jit(solution)/shard_map/ppermute | solution.py:496
  70.0 6.6 %collective-permute-start.3 = (f32[136,256]{1,0:T(8,128)S(1)}, f32[136,256]{1,0:T(8,128)S(1)}, u32[]{:S(2)}, u32[]{:S(2)}) collective-permute-start(f32[136,256]{1,0:T(8,128)S(1)} %get-tuple-element.15), channel_id=1, source_target_pairs={{0,96},{32,0},{64,32},{96,64},{1,97},{33,1},{65,33},{97,65},{2,98}... | collective-permute-start | bytes 417800 | tf_op jit(solution)/shard_map/ppermute | solution.py:496
  76.7 1.2 %copy-start = (f32[1,2,8,128]{3,1,2,0:T(2,128)}, f32[1,2,8,128]{3,1,2,0:T(2,128)S(1)}, u32[]{:S(2)}) copy-start(f32[1,2,8,128]{3,1,2,0:T(2,128)S(1)} %copy.15) | copy-start | bytes 24580
